TPU v7x, 32 devices: a whole 2x2x4 slice. The times are simulated.
32 devices in a mesh: ctx: 2 (over x), group: 4 (over z), replica: 4 (over y, core).
Axes of the slice: x: 2, y: 2, z: 4, core: 2. Of those that a mesh axis runs over, the one named last changes fastest.
Arguments:
- patches: bfloat16 [16, 2048, 768], P(('group', 'replica'), 'ctx'), may hold values from -6 to 6
- cotangent: bfloat16 [16, 2048, 768], P(('group', 'replica'), 'ctx'), may hold values from -6 to 6
- qkv_weight: bfloat16 [768, 2304], P('group'), may hold values from -0.21875 to 0.21875
- qkv_bias: bfloat16 [2304], P('group'), may hold values from -3 to 3
- query_gain: bfloat16 [64], P('group'), may hold values from 0.099609375 to 1.8984375
- query_shift: bfloat16 [64], P('group'), may hold values from -3 to 3
- key_gain: bfloat16 [64], P('group'), may hold values from 0.099609375 to 1.8984375
- norm_gain: bfloat16 [768], P('group'), may hold values from 0.099609375 to 1.8984375
- norm_shift: bfloat16 [768], P('group'), may hold values from -3 to 3
- out_weight: bfloat16 [768, 768], P('group'), may hold values from -1.25 to 1.25
- out_bias: bfloat16 [768], P('group'), may hold values from -3 to 3
- mlp_gain: bfloat16 [768], P('group'), may hold values from 0.099609375 to 1.8984375
- mlp_shift: bfloat16 [768], P('group'), may hold values from -3 to 3
- up_weight: bfloat16 [768, 3072], P('group'), may hold values from -0.21875 to 0.21875
- up_bias: bfloat16 [3072], P('group'), may hold values from -3 to 3
- down_weight: bfloat16 [3072, 768], P('group'), may hold values from -0.109375 to 0.109375
- down_bias: bfloat16 [768], P('group'), may hold values from -3 to 3
Outputs:
- layer_out: bfloat16 [16, 2048, 768], P(('group', 'replica'), 'ctx')
- grad_patches: float32 [16, 2048, 768], P(('group', 'replica'), 'ctx')
- grad_qkv_weight: float32 [768, 2304], P('group')
- grad_qkv_bias: float32 [2304], P('group')
- grad_query_gain: float32 [64], P('group')
- grad_query_shift: float32 [64], P('group')
- grad_key_gain: float32 [64], P('group')
- grad_norm_gain: float32 [768], P('group')
- grad_norm_shift: float32 [768], P('group')
- grad_out_weight: float32 [768, 768], P('group')
- grad_out_bias: float32 [768], P('group')
- grad_mlp_gain: float32 [768], P('group')
- grad_mlp_shift: float32 [768], P('group')
- grad_up_weight: float32 [768, 3072], P('group')
- grad_up_bias: float32 [3072], P('group')
- grad_down_weight: float32 [3072, 768], P('group')
- grad_down_bias: float32 [768], P('group')
All inputs are finite; a program needn't handle non-finite values.
Results may differ from a plain program's by a relative error of at most 0.019.
Values may be sent and summed in bfloat16 or wider, within the bound.
No kernel may reach another device: no remote copies, remote signals or barrier semaphores. Data moves between devices by JAX's collectives and lax.ppermute only.
A program may use at most 384 MiB of HBM per device.

v0:
```python
import jax
import jax.numpy as jnp
from jax import lax
from jax.sharding import PartitionSpec as P

HEADS = 12


EPS = 1e-06


def for_sending(x):
    return jax.tree.map(lambda a: a.astype(jnp.bfloat16) if a.dtype == jnp.float32 else a, x)


def layer_norm(value, gain, shift):
    mean = jnp.mean(value, -1, keepdims=True)
    cent = value - mean
    var = jnp.mean(cent * cent, -1, keepdims=True)
    rstd = lax.rsqrt(var + EPS)
    normed = cent * rstd
    return (normed * gain + shift, normed, rstd)


def norm_back(grad, normed, rstd, gain):
    scaled = grad * gain
    inner = (
        scaled
        - jnp.mean(scaled, -1, keepdims=True)
        - normed * jnp.mean(scaled * normed, -1, keepdims=True)
    )
    return inner * rstd


def gelu_parts(value):
    coeff = (2.0 / jnp.pi) ** 0.5
    inner = coeff * (value + 0.044715 * value * value * value)
    tangent = jnp.tanh(inner)
    output = 0.5 * value * (1.0 + tangent)
    slope = 0.5 * (1.0 + tangent) + 0.5 * value * (1.0 - tangent * tangent) * coeff * (
        1.0 + 3.0 * 0.044715 * value * value
    )
    return (output, slope)


def left_dot(left, right):
    return lax.dot_general(
        left, right, (((0,), (0,)), ((), ())), preferred_element_type=jnp.float32
    )


def right_dot(left, right):
    return lax.dot_general(
        left, right, (((1,), (1,)), ((), ())), preferred_element_type=jnp.float32
    )


def split_rows(value):
    local = value.shape[0]
    block = min(512, local)
    return value.reshape((local // block, block) + value.shape[1:])


def reorder_blocks(value, outer, inner):
    lead = value.shape[0]
    shaped = value.reshape((outer, inner, lead // (outer * inner)) + value.shape[1:])
    return jnp.swapaxes(shaped, 0, 1).reshape(value.shape)


def attend(items):
    query, keys, values = items
    local, heads, head = query.shape
    factor = head ** (-0.5)

    def one_block(query_blk):
        scores = (
            jnp.einsum("qhd,khd->hqk", query_blk, keys, preferred_element_type=jnp.float32) * factor
        )
        top = jnp.max(scores, -1, keepdims=True)
        total = jnp.sum(jnp.exp(scores - top), -1, keepdims=True)
        lse = top + jnp.log(total)
        probs = jnp.exp(scores - lse).astype(jnp.bfloat16)
        attn = jnp.einsum("hqk,khd->qhd", probs, values, preferred_element_type=jnp.float32)
        return (attn, lse)

    attn, lse = lax.map(one_block, split_rows(query))
    return (attn.reshape(local, heads, head), lse)


def attend_back(items):
    query, keys, values, lse, grad_attn = items
    local, heads, head = query.shape
    factor = head ** (-0.5)

    def one_block(carry, parts):
        query_blk, lse_blk, grad_blk = parts
        scores = (
            jnp.einsum("qhd,khd->hqk", query_blk, keys, preferred_element_type=jnp.float32) * factor
        )
        probs = jnp.exp(scores - lse_blk)
        grad_values = jnp.einsum(
            "hqk,qhd->khd", probs.astype(jnp.bfloat16), grad_blk, preferred_element_type=jnp.float32
        )
        grad_probs = jnp.einsum(
            "qhd,khd->hqk", grad_blk, values, preferred_element_type=jnp.float32
        )
        inner = jnp.sum(probs * grad_probs, -1, keepdims=True)
        grad_scores = (probs * (grad_probs - inner)).astype(jnp.bfloat16)
        grad_query = (
            jnp.einsum("hqk,khd->qhd", grad_scores, keys, preferred_element_type=jnp.float32)
            * factor
        )
        grad_keys = (
            jnp.einsum("hqk,qhd->khd", grad_scores, query_blk, preferred_element_type=jnp.float32)
            * factor
        )
        return ((carry[0] + grad_keys, carry[1] + grad_values), grad_query)

    zeros = jnp.zeros(keys.shape, jnp.float32)
    sums, grad_query = lax.scan(
        one_block, (zeros, zeros), (split_rows(query), lse, split_rows(grad_attn))
    )
    return (grad_query.reshape(local, heads, head), sums[0], sums[1])


def per_device(
    patches,
    cotangent,
    qkv_weight,
    qkv_bias,
    query_gain,
    query_shift,
    key_gain,
    norm_gain,
    norm_shift,
    out_weight,
    out_bias,
    mlp_gain,
    mlp_shift,
    up_weight,
    up_bias,
    down_weight,
    down_bias,
):
    shards = (
        qkv_weight,
        qkv_bias,
        query_gain,
        query_shift,
        key_gain,
        norm_gain,
        norm_shift,
        out_weight,
        out_bias,
        mlp_gain,
        mlp_shift,
        up_weight,
        up_bias,
        down_weight,
        down_bias,
    )
    whole = (
        lax.all_gather(shards[0], "group", axis=0, tiled=True),
        lax.all_gather(shards[1], "group", axis=0, tiled=True),
        lax.all_gather(shards[2], "group", axis=0, tiled=True),
        lax.all_gather(shards[3], "group", axis=0, tiled=True),
        lax.all_gather(shards[4], "group", axis=0, tiled=True),
        lax.all_gather(shards[5], "group", axis=0, tiled=True),
        lax.all_gather(shards[6], "group", axis=0, tiled=True),
        lax.all_gather(shards[7], "group", axis=0, tiled=True),
        lax.all_gather(shards[8], "group", axis=0, tiled=True),
        lax.all_gather(shards[9], "group", axis=0, tiled=True),
        lax.all_gather(shards[10], "group", axis=0, tiled=True),
        lax.all_gather(shards[11], "group", axis=0, tiled=True),
        lax.all_gather(shards[12], "group", axis=0, tiled=True),
        lax.all_gather(shards[13], "group", axis=0, tiled=True),
        lax.all_gather(shards[14], "group", axis=0, tiled=True),
    )
    (
        wqkv,
        bqkv,
        qgain,
        qshift,
        kgain,
        gain_one,
        shift_one,
        wout,
        bout,
        gain_two,
        shift_two,
        wup,
        bup,
        wdown,
        bdown,
    ) = whole
    images, local, width = patches.shape
    rows = images * local
    heads = HEADS
    head = width // heads
    inputs = patches.astype(jnp.float32).reshape(rows, width)
    normed_one, cent_one, rstd_one = layer_norm(
        inputs, gain_one.astype(jnp.float32), shift_one.astype(jnp.float32)
    )
    hidden = normed_one.astype(jnp.bfloat16)
    qkv = jnp.dot(hidden, wqkv, preferred_element_type=jnp.float32) + bqkv.astype(jnp.float32)
    query_pre = qkv[:, :width].reshape(rows, heads, head)
    keys_pre = qkv[:, width : 2 * width].reshape(rows, heads, head)
    query_f, query_n, query_r = layer_norm(
        query_pre, qgain.astype(jnp.float32), qshift.astype(jnp.float32)
    )
    keys_f, keys_n, keys_r = layer_norm(keys_pre, kgain.astype(jnp.float32), 0.0)
    query_b = query_f.astype(jnp.bfloat16).reshape(images, local, heads, head)
    keys_b = keys_f.astype(jnp.bfloat16).reshape(images, local, heads, head)
    values_b = qkv[:, 2 * width :].astype(jnp.bfloat16).reshape(images, local, heads, head)
    keys_all, values_all = (
        lax.all_gather(keys_b, "ctx", axis=1, tiled=True),
        lax.all_gather(values_b, "ctx", axis=1, tiled=True),
    )
    attn, lse = lax.map(attend, (query_b, keys_all, values_all))
    attn_b = attn.astype(jnp.bfloat16).reshape(rows, width)
    mixed = (
        inputs
        + jnp.dot(attn_b, wout, preferred_element_type=jnp.float32)
        + bout.astype(jnp.float32)
    )
    normed_two, cent_two, rstd_two = layer_norm(
        mixed, gain_two.astype(jnp.float32), shift_two.astype(jnp.float32)
    )
    hidden_two = normed_two.astype(jnp.bfloat16)
    upper = jnp.dot(hidden_two, wup, preferred_element_type=jnp.float32) + bup.astype(jnp.float32)
    active, slope = gelu_parts(upper)
    active_b = active.astype(jnp.bfloat16)
    output = (
        mixed
        + jnp.dot(active_b, wdown, preferred_element_type=jnp.float32)
        + bdown.astype(jnp.float32)
    )
    layer_out = output.astype(jnp.bfloat16).reshape(images, local, width)
    again = (
        lax.all_gather(shards[0], "group", axis=0, tiled=True),
        lax.all_gather(shards[1], "group", axis=0, tiled=True),
        lax.all_gather(shards[2], "group", axis=0, tiled=True),
        lax.all_gather(shards[3], "group", axis=0, tiled=True),
        lax.all_gather(shards[4], "group", axis=0, tiled=True),
        lax.all_gather(shards[5], "group", axis=0, tiled=True),
        lax.all_gather(shards[6], "group", axis=0, tiled=True),
        lax.all_gather(shards[7], "group", axis=0, tiled=True),
        lax.all_gather(shards[8], "group", axis=0, tiled=True),
        lax.all_gather(shards[9], "group", axis=0, tiled=True),
        lax.all_gather(shards[10], "group", axis=0, tiled=True),
        lax.all_gather(shards[11], "group", axis=0, tiled=True),
        lax.all_gather(shards[12], "group", axis=0, tiled=True),
        lax.all_gather(shards[13], "group", axis=0, tiled=True),
        lax.all_gather(shards[14], "group", axis=0, tiled=True),
    )
    (
        wqkv,
        bqkv,
        qgain,
        qshift,
        kgain,
        gain_one,
        shift_one,
        wout,
        bout,
        gain_two,
        shift_two,
        wup,
        bup,
        wdown,
        bdown,
    ) = again
    grad_out_f = cotangent.astype(jnp.float32).reshape(rows, width)
    grad_out_b = cotangent.reshape(rows, width)
    grad_wdown = left_dot(active_b, grad_out_b)
    grad_bdown = jnp.sum(grad_out_f, 0)
    grad_active = right_dot(grad_out_b, wdown)
    grad_upper = (grad_active * slope).astype(jnp.bfloat16)
    grad_wup = left_dot(hidden_two, grad_upper)
    grad_bup = jnp.sum(grad_upper.astype(jnp.float32), 0)
    grad_hidden_two = right_dot(grad_upper, wup)
    grad_gain_two = jnp.sum(grad_hidden_two * cent_two, 0)
    grad_shift_two = jnp.sum(grad_hidden_two, 0)
    grad_mixed = grad_out_f + norm_back(
        grad_hidden_two, cent_two, rstd_two, gain_two.astype(jnp.float32)
    )
    grad_branch = grad_mixed.astype(jnp.bfloat16)
    grad_wout = left_dot(attn_b, grad_branch)
    grad_bout = jnp.sum(grad_branch.astype(jnp.float32), 0)
    grad_attn = (
        right_dot(grad_branch, wout).astype(jnp.bfloat16).reshape(images, local, heads, head)
    )
    grad_query, keys_terms, values_terms = lax.map(
        attend_back, (query_b, keys_all, values_all, lse, grad_attn)
    )
    grad_keys, grad_values = (
        lax.psum_scatter(
            keys_terms.astype(jnp.bfloat16), "ctx", scatter_dimension=1, tiled=True
        ).astype(jnp.float32),
        lax.psum_scatter(
            values_terms.astype(jnp.bfloat16), "ctx", scatter_dimension=1, tiled=True
        ).astype(jnp.float32),
    )
    grad_query = grad_query.reshape(rows, heads, head)
    grad_keys = grad_keys.reshape(rows, heads, head)
    grad_qgain = jnp.sum(grad_query * query_n, (0, 1))
    grad_qshift = jnp.sum(grad_query, (0, 1))
    grad_kgain = jnp.sum(grad_keys * keys_n, (0, 1))
    grad_qpre = norm_back(grad_query, query_n, query_r, qgain.astype(jnp.float32)).reshape(
        rows, width
    )
    grad_kpre = norm_back(grad_keys, keys_n, keys_r, kgain.astype(jnp.float32)).reshape(rows, width)
    grad_qkv = jnp.concatenate([grad_qpre, grad_kpre, grad_values.reshape(rows, width)], 1).astype(
        jnp.bfloat16
    )
    grad_wqkv = left_dot(hidden, grad_qkv)
    grad_bqkv = jnp.sum(grad_qkv.astype(jnp.float32), 0)
    grad_hidden = right_dot(grad_qkv, wqkv)
    grad_gain_one = jnp.sum(grad_hidden * cent_one, 0)
    grad_shift_one = jnp.sum(grad_hidden, 0)
    grad_inputs = grad_mixed + norm_back(
        grad_hidden, cent_one, rstd_one, gain_one.astype(jnp.float32)
    )
    terms = (
        grad_wqkv,
        grad_bqkv,
        grad_qgain,
        grad_qshift,
        grad_kgain,
        grad_gain_one,
        grad_shift_one,
        grad_wout,
        grad_bout,
        grad_gain_two,
        grad_shift_two,
        grad_wup,
        grad_bup,
        grad_wdown,
        grad_bdown,
    )
    groups = lax.axis_size("group")
    halves = lax.axis_size("ctx")
    placed = tuple((reorder_blocks(term, groups, halves) for term in terms))
    shares = jax.tree.map(
        lambda part: part.astype(jnp.float32),
        lax.psum_scatter(for_sending(placed), ("ctx", "group"), scatter_dimension=0, tiled=True),
    )
    summed = jax.tree.map(
        lambda part: part.astype(jnp.float32), lax.psum(for_sending(shares), "replica")
    )
    totals = jax.tree.map(
        lambda part, own: part.astype(own.dtype),
        lax.all_gather(for_sending(summed), "ctx", axis=0, tiled=True),
        summed,
    )
    return (layer_out, grad_inputs.reshape(images, local, width)) + tuple(totals)


def solution(mesh):
    return jax.shard_map(
        per_device,
        mesh=mesh,
        in_specs=(
            P(("group", "replica"), "ctx", None),
            P(("group", "replica"), "ctx", None),
            P("group", None),
            P("group"),
            P("group"),
            P("group"),
            P("group"),
            P("group"),
            P("group"),
            P("group", None),
            P("group"),
            P("group"),
            P("group"),
            P("group", None),
            P("group"),
            P("group", None),
            P("group"),
        ),
        out_specs=(
            P(("group", "replica"), "ctx", None),
            P(("group", "replica"), "ctx", None),
            P("group", None),
            P("group"),
            P("group"),
            P("group"),
            P("group"),
            P("group"),
            P("group"),
            P("group", None),
            P("group"),
            P("group"),
            P("group"),
            P("group", None),
            P("group"),
            P("group", None),
            P("group"),
        ),
        check_vma=False,
    )
```

profile of v0, /device:TPU:0, one launch (start us, length us, event | category | flops | bytes accessed | tf_op | source)
XLA Modules:
  0.0 1350.5 jit_solution(2778765949011613362)
XLA Ops:
  19.6 22.3 %all-reduce.34 = (bf16[768]{0:T(1024)(128)(2,1)}, bf16[64]{0:T(256)(128)(2,1)S(1)}, bf16[64]{0:T(256)(128)(2,1)S(1)}, bf16[768]{0:T(1024)(128)(2,1)S(1)}, bf16[7...) all-reduce(bf16[768]{0:T(1024)(128)(2,1)S(1)} %dynamic-update-slice, ...), channel_id=1, replica_groups=mesh['ctx'=2,'group'=4,'replica'=4] {'group'}, use_global_device_ids=true, to_apply=%add.9 | all-reduce | flops 7104 | bytes 28416
  46.0 37.2 %all-gather.11.cloned.1.call-done = bf16[768,2304]{1,0:T(8,128)(2,1)} async-done(((bf16[192,2304]{1,0:T(8,128)(2,1)}), bf16[768,2304]{1,0:T(8,128)(2,1)}) %all-gather.11.cloned.1.call-update) | async-done | bytes 3538960 | tf_op jit(solution)/shard_map/all_gather | solution.py:163
  140.7 44.7 %all-gather.13.cloned.1.call-done = bf16[1,2048,12,64]{1,3,2,0:T(8,128)(2,1)} async-done(((bf16[1,1024,12,64]{1,3,2,0:T(8,128)(2,1)}), bf16[1,2048,12,64]{1,3,2,0:T(8,128)(2,1)}) %all-gather.13.cloned.1.call-update) | async-done | bytes 3145744 | tf_op jit(solution)/shard_map/all_gather | solution.py:216
  185.4 122.8 %while.49 = (s32[]{:T(128)}, bf16[2,512,12,64]{1,3,2,0:T(8,128)(2,1)S(1)}, f32[2,12,512,1]{2,1,3,0:T(8,128)S(1)}, bf16[2,512,12,64]{1,3,2,0:T(8,128)(2,1)S(1)}, ...) while((s32[]{:T(128)}, bf16[2,512,12,64]{1,3,2,0:T(8,128)(2,1)S(1)}, ...), condition=%wide.region_9.10_spmd.clone, body=%wide.region_6.9_spmd.sunk.clone | while | flops 3321882624 | bytes 172466288 | solution.py:86
  185.4 21.8 %multiply_reduce_fusion.17 = (f32[12,512]{1,0:T(8,128)S(1)}, f32[12,512,2048]{2,1,0:T(8,128)}) fusion(bf16[2048,12,64]{0,2,1:T(8,128)(2,1)} %get-tuple-element.575, bf16[2,512,12,64]{1,3,2,0:T(8,128)(2,1)S(1)} %get-tuple-element.574, s32[]{:T(128)S(6)} %copy.248), kind=kOutput, calls=%fused_computation.2.clone.1.clone | convolution fusion | flops 1635772416 | bytes 54288388 | tf_op jit(solution)/shard_map/while/body/eval_jaxpr/while/body/eval_jaxpr/qhd,khd->hqk/dot_general | solution.py:77
  207.2 21.2 %exponential_reduce_fusion.3 = f32[12,512]{1,0:T(8,128)S(1)} fusion(f32[12,512,2048]{2,1,0:T(8,128)} %get-tuple-element.525, f32[12,512]{1,0:T(8,128)S(1)} %get-tuple-element.526), kind=kLoop, calls=%fused_computation.1.clone.1.clone | loop fusion | flops 37742592 | bytes 50380800 | tf_op jit(solution)/shard_map/while/body/eval_jaxpr/while/body/eval_jaxpr/reduce_sum | solution.py:80
  228.4 18.8 %bitcast_dynamic-update-slice_fusion.10 = bf16[2,512,12,64]{1,3,2,0:T(8,128)(2,1)S(1)} fusion(bf16[2,512,12,64]{1,3,2,0:T(8,128)(2,1)S(1)} %get-tuple-element.566, s32[]{:T(128)S(6)} %copy.248, bf16[2048,12,64]{0,2,1:T(8,128)(2,1)S(1)} %copy-done.1, f32[12,512,2048]{2,1,0:T(8,128)} %get-tuple-element.525, f32[12,512]{1,0:T(8,128)S(1)} %get-tuple-element.527), kind=kOutput, calls=%fused_computation.4.clone.1.clone | convolution fusion | flops 1648361472 | bytes 55083012 | tf_op jit(solution)/shard_map/while/body/eval_jaxpr/while/body/eval_jaxpr/hqk,khd->qhd/dot_general | solution.py:83
  247.2 21.6 %multiply_reduce_fusion.17 = (f32[12,512]{1,0:T(8,128)S(1)}, f32[12,512,2048]{2,1,0:T(8,128)}) fusion(bf16[2048,12,64]{0,2,1:T(8,128)(2,1)} %get-tuple-element.575, bf16[2,512,12,64]{1,3,2,0:T(8,128)(2,1)S(1)} %get-tuple-element.574, s32[]{:T(128)S(6)} %copy.248), kind=kOutput, calls=%fused_computation.2.clone.1.clone | convolution fusion | flops 1635772416 | bytes 54288388 | tf_op jit(solution)/shard_map/while/body/eval_jaxpr/while/body/eval_jaxpr/qhd,khd->hqk/dot_general | solution.py:77
  268.8 20.8 %exponential_reduce_fusion.3 = f32[12,512]{1,0:T(8,128)S(1)} fusion(f32[12,512,2048]{2,1,0:T(8,128)} %get-tuple-element.525, f32[12,512]{1,0:T(8,128)S(1)} %get-tuple-element.526), kind=kLoop, calls=%fused_computation.1.clone.1.clone | loop fusion | flops 37742592 | bytes 50380800 | tf_op jit(solution)/shard_map/while/body/eval_jaxpr/while/body/eval_jaxpr/reduce_sum | solution.py:80
  289.6 18.6 %bitcast_dynamic-update-slice_fusion.10 = bf16[2,512,12,64]{1,3,2,0:T(8,128)(2,1)S(1)} fusion(bf16[2,512,12,64]{1,3,2,0:T(8,128)(2,1)S(1)} %get-tuple-element.566, s32[]{:T(128)S(6)} %copy.248, bf16[2048,12,64]{0,2,1:T(8,128)(2,1)S(1)} %copy-done.1, f32[12,512,2048]{2,1,0:T(8,128)} %get-tuple-element.525, f32[12,512]{1,0:T(8,128)S(1)} %get-tuple-element.527), kind=kOutput, calls=%fused_computation.4.clone.1.clone | convolution fusion | flops 1648361472 | bytes 55083012 | tf_op jit(solution)/shard_map/while/body/eval_jaxpr/while/body/eval_jaxpr/hqk,khd->qhd/dot_general | solution.py:83
  320.3 15.7 %fusion.39 = (bf16[3072,1024]{0,1:T(8,128)(2,1)}, f32[1024,3072]{1,0:T(8,128)}) fusion(f32[3072]{0:T(1024)S(1)} %bitcast.320, bf16[768,3072]{1,0:T(8,128)(2,1)} %all-gather.19.cloned.1.call-done, f32[1024,768]{0,1:T(8,128)} %copy-done.10, f32[768]{0:T(1024)S(1)} %copy-done.63, f32[768]{0:T(1024)S(1)} %copy-done.54, f32[1024]{0:T(1024)S(1)} %add_rsqrt_fusion.2, ...), kind=kOutput, calls=%fused_computation.52 | convolution fusion | flops 4867227648 | bytes 26765312 | tf_op jit(solution)/shard_map/dot_general | solution.py:230
  336.1 60.3 %all-gather.21.cloned.1.call-done = bf16[3072,768]{1,0:T(8,128)(2,1)} async-done(((bf16[768,768]{1,0:T(8,128)(2,1)}), bf16[3072,768]{1,0:T(8,128)(2,1)}) %all-gather.21.cloned.1.call-update) | async-done | bytes 4718608 | tf_op jit(solution)/shard_map/all_gather | solution.py:176
  396.4 14.8 %fusion.89 = (bf16[3072]{0:T(1024)(128)(2,1)}, bf16[1024,3072]{1,0:T(8,128)(2,1)S(1)}) fusion(f32[1024,3072]{1,0:T(8,128)} %get-tuple-element.405, f32[3072]{0:T(1024)S(1)} %bitcast.321, bf16[3072,768]{1,0:T(8,128)(2,1)} %all-gather.21.cloned.1.call-done, bf16[1,1024,768]{2,1,0:T(8,128)(2,1)S(1)} %copy-done.24), kind=kOutput, calls=%fused_computation.149 | convolution fusion | flops 4897895424 | bytes 25184256 | tf_op jit(solution)/shard_map/dot_general | solution.py:53
  439.4 296.6 %while.50 = (s32[]{:T(128)}, f32[2048,12,64]{0,2,1:T(8,128)}, f32[2048,12,64]{0,2,1:T(8,128)}, f32[2,512,12,64]{1,3,2,0:T(8,128)}, bf16[2,512,12,64]{1,3,2,0:T(8...) while((s32[]{:T(128)}, f32[2048,12,64]{0,2,1:T(8,128)}, ...), condition=%wide.region_16.17_spmd.clone.clone, body=%wide.region_14.16_spmd.clone.sunk.clone | while | flops 8212310016 | bytes 416981088 | solution.py:120
  439.8 20.5 %fusion.147 = f32[12,512,2048]{2,1,0:T(8,128)} fusion(bf16[2048,12,64]{0,2,1:T(8,128)(2,1)S(1)} %get-tuple-element.600, bf16[2,512,12,64]{1,3,2,0:T(8,128)(2,1)} %get-tuple-element.599, s32[]{:T(128)S(6)} %copy.258), kind=kOutput, calls=%fused_computation.26.clone.1.clone | convolution fusion | flops 1610612736 | bytes 54263812 | tf_op jit(solution)/shard_map/while/body/eval_jaxpr/while/body/eval_jaxpr/qhd,khd->hqk/dot_general | solution.py:98
  460.3 21.8 %bitcast_add_fusion.7 = f32[2048,12,64]{0,2,1:T(8,128)} fusion(f32[2048,12,64]{0,2,1:T(8,128)} %get-tuple-element.588, f32[12,512,2048]{2,1,0:T(8,128)} %fusion.147, f32[12,512]{1,0:T(8,128)S(1)} %dynamic-slice_bitcast_fusion.3, pred[]{:T(512)S(6)} %compare.4, bf16[2,512,12,64]{1,3,2,0:T(8,128)(2,1)} %get-tuple-element.602, s32[]{:T(128)S(6)} %copy.258), kind=kOutput, calls=%fused_computation.19.clone.1.clone | convolution fusion | flops 1651507200 | bytes 63725572 | tf_op jit(solution)/shard_map/while/body/eval_jaxpr/while/body/eval_jaxpr/hqk,qhd->khd/dot_general | solution.py:101
  482.1 34.3 %multiply_reduce_fusion.18 = (f32[12,512]{1,0:T(8,128)S(1)}, f32[12,512,2048]{2,1,0:T(8,128)}) fusion(f32[12,512,2048]{2,1,0:T(8,128)} %fusion.147, f32[12,512]{1,0:T(8,128)S(1)} %dynamic-slice_bitcast_fusion.3, bf16[2048,12,64]{0,2,1:T(8,128)(2,1)} %get-tuple-element.603, bf16[2,512,12,64]{1,3,2,0:T(8,128)(2,1)} %get-tuple-element.602, ...), kind=kOutput, calls=%fused_computation.13.clone.1.clone | convolution fusion | flops 1660938240 | bytes 104644608 | tf_op jit(solution)/shard_map/while/body/eval_jaxpr/while/body/eval_jaxpr/qhd,khd->hqk/dot_general | solution.py:104
  516.3 40.4 %multiply_convert_fusion.12 = bf16[12,512,2048]{2,1,0:T(8,128)(2,1)} fusion(f32[12,512,2048]{2,1,0:T(8,128)} %get-tuple-element.546, f32[12,512,2048]{2,1,0:T(8,128)} %fusion.147, f32[12,512]{1,0:T(8,128)S(1)} %get-tuple-element.547, f32[12,512]{1,0:T(8,128)S(1)} %dynamic-slice_bitcast_fusion.3), kind=kLoop, calls=%fused_computation.12.clone.1.clone | loop fusion | flops 62914560 | bytes 125878272 | tf_op jit(solution)/shard_map/while/body/eval_jaxpr/while/body/eval_jaxpr/convert_element_type | solution.py:108
  556.7 13.7 %bitcast_dynamic-update-slice_fusion.11 = f32[2,512,12,64]{1,3,2,0:T(8,128)} fusion(f32[2,512,12,64]{1,3,2,0:T(8,128)} %get-tuple-element.589, s32[]{:T(128)S(6)} %copy.258, bf16[12,512,2048]{2,1,0:T(8,128)(2,1)} %multiply_convert_fusion.12, bf16[2048,12,64]{0,2,1:T(8,128)(2,1)S(1)} %get-tuple-element.600), kind=kOutput, calls=%fused_computation.21.clone.1.clone | convolution fusion | flops 1611005952 | bytes 29884420 | tf_op jit(solution)/shard_map/while/body/eval_jaxpr/while/body/eval_jaxpr/hqk,khd->qhd/dot_general | solution.py:110
  570.4 15.6 %bitcast_add_fusion.6 = f32[2048,12,64]{0,2,1:T(8,128)} fusion(f32[2048,12,64]{0,2,1:T(8,128)} %get-tuple-element.587, bf16[12,512,2048]{2,1,0:T(8,128)(2,1)} %multiply_convert_fusion.12, pred[]{:T(512)S(6)} %compare.4, bf16[2,512,12,64]{1,3,2,0:T(8,128)(2,1)} %get-tuple-element.599, s32[]{:T(128)S(6)} %copy.258), kind=kOutput, calls=%fused_computation.20.clone.1.clone | convolution fusion | flops 1615331328 | bytes 38535172 | tf_op jit(solution)/shard_map/while/body/eval_jaxpr/while/body/eval_jaxpr/hqk,qhd->khd/dot_general | solution.py:114
  586.0 20.5 %fusion.147 = f32[12,512,2048]{2,1,0:T(8,128)} fusion(bf16[2048,12,64]{0,2,1:T(8,128)(2,1)S(1)} %get-tuple-element.600, bf16[2,512,12,64]{1,3,2,0:T(8,128)(2,1)} %get-tuple-element.599, s32[]{:T(128)S(6)} %copy.258), kind=kOutput, calls=%fused_computation.26.clone.1.clone | convolution fusion | flops 1610612736 | bytes 54263812 | tf_op jit(solution)/shard_map/while/body/eval_jaxpr/while/body/eval_jaxpr/qhd,khd->hqk/dot_general | solution.py:98
  606.5 23.5 %bitcast_add_fusion.7 = f32[2048,12,64]{0,2,1:T(8,128)} fusion(f32[2048,12,64]{0,2,1:T(8,128)} %get-tuple-element.588, f32[12,512,2048]{2,1,0:T(8,128)} %fusion.147, f32[12,512]{1,0:T(8,128)S(1)} %dynamic-slice_bitcast_fusion.3, pred[]{:T(512)S(6)} %compare.4, bf16[2,512,12,64]{1,3,2,0:T(8,128)(2,1)} %get-tuple-element.602, s32[]{:T(128)S(6)} %copy.258), kind=kOutput, calls=%fused_computation.19.clone.1.clone | convolution fusion | flops 1651507200 | bytes 63725572 | tf_op jit(solution)/shard_map/while/body/eval_jaxpr/while/body/eval_jaxpr/hqk,qhd->khd/dot_general | solution.py:101
  630.0 34.3 %multiply_reduce_fusion.18 = (f32[12,512]{1,0:T(8,128)S(1)}, f32[12,512,2048]{2,1,0:T(8,128)}) fusion(f32[12,512,2048]{2,1,0:T(8,128)} %fusion.147, f32[12,512]{1,0:T(8,128)S(1)} %dynamic-slice_bitcast_fusion.3, bf16[2048,12,64]{0,2,1:T(8,128)(2,1)} %get-tuple-element.603, bf16[2,512,12,64]{1,3,2,0:T(8,128)(2,1)} %get-tuple-element.602, ...), kind=kOutput, calls=%fused_computation.13.clone.1.clone | convolution fusion | flops 1660938240 | bytes 104644608 | tf_op jit(solution)/shard_map/while/body/eval_jaxpr/while/body/eval_jaxpr/qhd,khd->hqk/dot_general | solution.py:104
  664.3 40.4 %multiply_convert_fusion.12 = bf16[12,512,2048]{2,1,0:T(8,128)(2,1)} fusion(f32[12,512,2048]{2,1,0:T(8,128)} %get-tuple-element.546, f32[12,512,2048]{2,1,0:T(8,128)} %fusion.147, f32[12,512]{1,0:T(8,128)S(1)} %get-tuple-element.547, f32[12,512]{1,0:T(8,128)S(1)} %dynamic-slice_bitcast_fusion.3), kind=kLoop, calls=%fused_computation.12.clone.1.clone | loop fusion | flops 62914560 | bytes 125878272 | tf_op jit(solution)/shard_map/while/body/eval_jaxpr/while/body/eval_jaxpr/convert_element_type | solution.py:108
  704.7 13.7 %bitcast_dynamic-update-slice_fusion.11 = f32[2,512,12,64]{1,3,2,0:T(8,128)} fusion(f32[2,512,12,64]{1,3,2,0:T(8,128)} %get-tuple-element.589, s32[]{:T(128)S(6)} %copy.258, bf16[12,512,2048]{2,1,0:T(8,128)(2,1)} %multiply_convert_fusion.12, bf16[2048,12,64]{0,2,1:T(8,128)(2,1)S(1)} %get-tuple-element.600), kind=kOutput, calls=%fused_computation.21.clone.1.clone | convolution fusion | flops 1611005952 | bytes 29884420 | tf_op jit(solution)/shard_map/while/body/eval_jaxpr/while/body/eval_jaxpr/hqk,khd->qhd/dot_general | solution.py:110
  718.4 17.4 %bitcast_add_fusion.6 = f32[2048,12,64]{0,2,1:T(8,128)} fusion(f32[2048,12,64]{0,2,1:T(8,128)} %get-tuple-element.587, bf16[12,512,2048]{2,1,0:T(8,128)(2,1)} %multiply_convert_fusion.12, pred[]{:T(512)S(6)} %compare.4, bf16[2,512,12,64]{1,3,2,0:T(8,128)(2,1)} %get-tuple-element.599, s32[]{:T(128)S(6)} %copy.258), kind=kOutput, calls=%fused_computation.20.clone.1.clone | convolution fusion | flops 1615331328 | bytes 38535172 | tf_op jit(solution)/shard_map/while/body/eval_jaxpr/while/body/eval_jaxpr/hqk,qhd->khd/dot_general | solution.py:114
  867.7 29.7 %reduce-scatter.13.cloned.1.call-done = bf16[96,768]{1,0:T(8,128)(2,1)} async-done(((bf16[768,768]{1,0:T(8,128)(2,1)}), bf16[96,768]{1,0:T(8,128)(2,1)}) %reduce-scatter.13.cloned.1.call-update) | async-done | bytes 147472 | tf_op jit(solution)/shard_map/reduce_scatter | solution.py:346
  897.4 98.2 %reduce-scatter.17.cloned.1.call-done = bf16[384,768]{1,0:T(8,128)(2,1)} async-done(((bf16[3072,768]{1,0:T(8,128)(2,1)}), bf16[384,768]{1,0:T(8,128)(2,1)}) %reduce-scatter.17.cloned.1.call-update) | async-done | bytes 589840 | tf_op jit(solution)/shard_map/reduce_scatter | solution.py:346
  995.6 99.0 %reduce-scatter.15.cloned.1.call-done = bf16[96,3072]{1,0:T(8,128)(2,1)} async-done(((bf16[768,3072]{1,0:T(8,128)(2,1)}), bf16[96,3072]{1,0:T(8,128)(2,1)}) %reduce-scatter.15.cloned.1.call-update) | async-done | bytes 589840 | tf_op jit(solution)/shard_map/reduce_scatter | solution.py:346
  1094.5 82.6 %reduce-scatter.11.cloned.1.call-done = bf16[96,2304]{1,0:T(8,128)(2,1)} async-done(((bf16[768,2304]{1,0:T(8,128)(2,1)}), bf16[96,2304]{1,0:T(8,128)(2,1)}) %reduce-scatter.11.cloned.1.call-update) | async-done | bytes 442384 | tf_op jit(solution)/shard_map/reduce_scatter | solution.py:346
  1194.8 30.7 %all-reduce.38.cloned.1.call-done = (bf16[96,2304]{1,0:T(8,128)(2,1)}, bf16[96,768]{1,0:T(8,128)(2,1)}, bf16[96,3072]{1,0:T(8,128)(2,1)}, bf16[384,768]{1,0:T(8,128)(2,1)}) async-done(((bf16[96,2304]{1,0:T(8,128)(2,1)}, bf16[96,768]{1,0:T(8,128)(2,1)}, bf16[96,3072]{1,0:T(8,128)(2,1)}, bf16[384,768]{1,0:T(8,128)(2,1)}), (bf16[96,2304]{1,0:T(8,128)(2,1)}, bf16[96,768]{1,0:T(8,128)(2,1)}, ...) | async-done | bytes 1769488 | tf_op jit(solution)/shard_map/psum | solution.py:349
  1243.0 37.6 %all-reduce.31 = (bf16[2304]{0:T(1024)(128)(2,1)S(1)}, bf16[64]{0:T(256)(128)(2,1)S(1)}, bf16[64]{0:T(256)(128)(2,1)S(1)}, bf16[64]{0:T(256)(128)(2,1)S(1)}, bf1...) all-reduce(bf16[2304]{0:T(1024)(128)(2,1)S(1)} %convert_element_typ, ...), channel_id=5, replica_groups=mesh['ctx'=2,'group'=4,'replica'=4] {'ctx','group'}, use_global_device_ids=true, to_apply=%region_28.29.clone | all-reduce | flops 10176 | bytes 40704
  (434 shorter events, 336.7 us)
Async XLA Ops:
  7.2 76.0 %all-gather.11.cloned.1.call-start = ((), (), s32[]{:S(2)}) async-start(), calls=%async_computation.6 | async-start | bytes 4423680 | tf_op jit(solution)/shard_map/all_gather | solution.py:163
  7.9 132.8 %all-gather.15.cloned.1.call-start = ((), (), s32[]{:S(2)}) async-start(), calls=%async_computation.8 | async-start | bytes 4718592 | tf_op jit(solution)/shard_map/all_gather | solution.py:217
  41.9 52.8 %copy-start.75 = (bf16[64]{0:T(256)(128)(2,1)}, bf16[64]{0:T(256)(128)(2,1)S(1)}, u32[]{:S(2)}) copy-start(bf16[64]{0:T(256)(128)(2,1)S(1)} %get-tuple-element.375) | copy-start | bytes 388
  41.9 68.2 %copy-start.73 = (bf16[64]{0:T(256)(128)(2,1)}, bf16[64]{0:T(256)(128)(2,1)S(1)}, u32[]{:S(2)}) copy-start(bf16[64]{0:T(256)(128)(2,1)S(1)} %get-tuple-element.371) | copy-start | bytes 388
  46.0 43.1 %copy-start.26 = (bf16[1024,768]{0,1:T(8,128)(2,1)}, bf16[1024,768]{0,1:T(8,128)(2,1)S(1)}, u32[]{:S(2)}) copy-start(bf16[1024,768]{0,1:T(8,128)(2,1)S(1)} %fusion.54) | copy-start | bytes 4718596
  94.6 90.8 %all-gather.13.cloned.1.call-start = ((), (), s32[]{:S(2)}) async-start(), calls=%async_computation.7 | async-start | bytes 4718592 | tf_op jit(solution)/shard_map/all_gather | solution.py:216
  106.9 19.2 %copy-start.23 = (bf16[1,1024,768]{2,1,0:T(8,128)(2,1)S(1)}, bf16[1,1024,768]{2,1,0:T(8,128)(2,1)}, u32[]{:S(2)}) copy-start(bf16[1,1024,768]{2,1,0:T(8,128)(2,1)} %param.22) | copy-start | bytes 4718596
  107.0 207.6 %all-gather.17.cloned.1.call-start = ((), (), s32[]{:S(2)}) async-start(), calls=%async_computation.9 | async-start | bytes 1474560 | tf_op jit(solution)/shard_map/all_gather | solution.py:170
  107.6 212.7 %all-gather.19.cloned.1.call-start = ((), (), s32[]{:S(2)}) async-start(), calls=%async_computation.10 | async-start | bytes 5898240 | tf_op jit(solution)/shard_map/all_gather | solution.py:174
  108.1 288.3 %all-gather.21.cloned.1.call-start = ((), (), s32[]{:S(2)}) async-start(), calls=%async_computation.11 | async-start | bytes 5898240 | tf_op jit(solution)/shard_map/all_gather | solution.py:176
  108.7 716.9 %reduce-scatter.7.cloned.1.call-start = ((), (), s32[]{:S(2)}) async-start(), calls=%async_computation.12 | async-start | bytes 4718592 | tf_op jit(solution)/shard_map/reduce_scatter | solution.py:297
  110.1 24.8 %copy-start.71 = (f32[64]{0:T(128)}, f32[64]{0:T(128)S(1)}, u32[]{:S(2)}) copy-start(f32[64]{0:T(128)S(1)} %convert_element_type.391) | copy-start | bytes 772
  136.1 49.3 %copy-start.29 = (bf16[2,512,12,64]{1,3,2,0:T(8,128)(2,1)S(1)}, bf16[2,512,12,64]{1,3,2,0:T(8,128)(2,1)}, u32[]{:S(2)}) copy-start(bf16[2,512,12,64]{1,3,2,0:T(8,128)(2,1)} %broadcast_convert_fusion) | copy-start | bytes 4718596
  207.1 21.2 %copy-start.1 = (bf16[2048,12,64]{0,2,1:T(8,128)(2,1)S(1)}, bf16[2048,12,64]{0,2,1:T(8,128)(2,1)}, u32[]{:S(2)}) copy-start(bf16[2048,12,64]{0,2,1:T(8,128)(2,1)} %get-tuple-element.576) | copy-start | bytes 9437188 | tf_op jit(solution)/shard_map/while/body/eval_jaxpr/while
  268.8 20.8 %copy-start.1 = (bf16[2048,12,64]{0,2,1:T(8,128)(2,1)S(1)}, bf16[2048,12,64]{0,2,1:T(8,128)(2,1)}, u32[]{:S(2)}) copy-start(bf16[2048,12,64]{0,2,1:T(8,128)(2,1)} %get-tuple-element.576) | copy-start | bytes 9437188 | tf_op jit(solution)/shard_map/while/body/eval_jaxpr/while
  318.3 107.5 %copy-start.52 = (f32[1024]{0:T(1024)}, f32[1024]{0:T(1024)S(1)}, u32[]{:S(2)}) copy-start(f32[1024]{0:T(1024)S(1)} %broadcast_multiply_fusion.8) | copy-start | bytes 12292
  320.3 105.5 %copy-start.56 = (f32[1024]{0:T(1024)}, f32[1024]{0:T(1024)S(1)}, u32[]{:S(2)}) copy-start(f32[1024]{0:T(1024)S(1)} %add_rsqrt_fusion.2) | copy-start | bytes 12292
  320.3 76.1 %copy-start.24 = (bf16[1,1024,768]{2,1,0:T(8,128)(2,1)S(1)}, bf16[1,1024,768]{2,1,0:T(8,128)(2,1)}, u32[]{:S(2)}) copy-start(bf16[1,1024,768]{2,1,0:T(8,128)(2,1)} %param.22) | copy-start | bytes 4718596
  396.4 14.8 %copy-start.77 = (bf16[768,3072]{1,0:T(8,128)(2,1)S(1)}, bf16[768,3072]{1,0:T(8,128)(2,1)}, u32[]{:S(2)}) copy-start(bf16[768,3072]{1,0:T(8,128)(2,1)} %all-gather.19.cloned.1.call-done) | copy-start | bytes 14155780
  741.0 96.1 %reduce-scatter.9.cloned.1.call-start = ((), (), s32[]{:S(2)}) async-start(), calls=%async_computation.13 | async-start | bytes 4718592 | tf_op jit(solution)/shard_map/reduce_scatter | solution.py:300
  746.3 151.1 %reduce-scatter.13.cloned.1.call-start = ((), (), s32[]{:S(2)}) async-start(), calls=%async_computation.15 | async-start | bytes 1327104 | tf_op jit(solution)/shard_map/reduce_scatter | solution.py:346
  752.3 243.3 %reduce-scatter.17.cloned.1.call-start = ((), (), s32[]{:S(2)}) async-start(), calls=%async_computation.18 | async-start | bytes 5308416 | tf_op jit(solution)/shard_map/reduce_scatter | solution.py:346
  771.8 322.7 %reduce-scatter.15.cloned.1.call-start = ((), (), s32[]{:S(2)}) async-start(), calls=%async_computation.16 | async-start | bytes 5308416 | tf_op jit(solution)/shard_map/reduce_scatter | solution.py:346
  784.8 392.3 %reduce-scatter.11.cloned.1.call-start = ((), (), s32[]{:S(2)}) async-start(), calls=%async_computation.14 | async-start | bytes 3981312 | tf_op jit(solution)/shard_map/reduce_scatter | solution.py:346
  859.4 317.7 %copy-start.13 = (f32[1024,768]{0,1:T(8,128)S(1)}, f32[1024,768]{0,1:T(8,128)}, u32[]{:S(2)}) copy-start(f32[1024,768]{0,1:T(8,128)} %copy-done.10) | copy-start | bytes 9437188
  859.5 317.7 %copy-start.59 = (f32[4,1,768]{2,1,0:T(1,128)S(1)}, f32[4,1,768]{2,1,0:T(1,128)}, u32[]{:S(2)}) copy-start(f32[4,1,768]{2,1,0:T(1,128)} %convert_element_type.483) | copy-start | bytes 36868
  859.5 366.0 %all-reduce.38.cloned.1.call-start = ((), (), s32[]{:S(2)}) async-start(), calls=%async_computation.20 | async-start | bytes 3538944 | tf_op jit(solution)/shard_map/psum | solution.py:349
  1177.1 160.9 %all-gather.25.cloned.1.call-start = ((), (), s32[]{:S(2)}) async-start(), calls=%async_computation.19 | async-start | bytes 1769472 | tf_op jit(solution)/shard_map/all_gather | solution.py:353
  1177.2 14.0 %copy-start.62 = (bf16[3072]{0:T(1024)(128)(2,1)S(1)}, bf16[3072]{0:T(1024)(128)(2,1)}, u32[]{:S(2)}) copy-start(bf16[3072]{0:T(1024)(128)(2,1)} %get-tuple-element.410) | copy-start | bytes 18436
  1188.7 36.9 %copy-start.20 = (bf16[1024,768]{1,0:T(8,128)(2,1)S(1)}, bf16[1024,768]{1,0:T(8,128)(2,1)}, u32[]{:S(2)}) copy-start(bf16[1024,768]{1,0:T(8,128)(2,1)} %copy-done.19) | copy-start | bytes 4718596
  1188.7 36.9 %copy-start.22 = (bf16[1024,768]{1,0:T(8,128)(2,1)S(1)}, bf16[1024,768]{1,0:T(8,128)(2,1)}, u32[]{:S(2)}) copy-start(bf16[1024,768]{1,0:T(8,128)(2,1)} %copy-done.21) | copy-start | bytes 4718596
  1225.5 115.3 %all-gather.23.cloned.1.call-start = ((), (), s32[]{:S(2)}) async-start(), calls=%async_computation.17 | async-start | bytes 1769472 | tf_op jit(solution)/shard_map/all_gather | solution.py:353
  (66 other events, 242.8 us)
Sparse Core Ops, SparseCore 0:
  9.6 73.6 all-gather.10
  94.7 43.5 all-gather.14
  140.4 44.8 all-gather.12
  186.8 30.2 all-gather.16
  218.5 88.6 all-gather.18
  308.6 87.7 all-gather.20
  741.1 41.8 reduce-scatter.6
  785.2 43.3 reduce-scatter.8
  832.6 64.6 reduce-scatter.12
  900.9 94.6 reduce-scatter.16
  999.2 95.2 reduce-scatter.14
  1098.0 79.0 reduce-scatter.10
  1179.7 45.7 all-reduce.37
  1226.9 22.8 all-gather.24
  1305.3 23.6 all-gather.22
where the time goes:
time: 1360 us; the launch traced here: 1350 us
  waiting for transfers between devices  485 us (36%)
  matrix products  388 us (29%)
  other arithmetic  207 us (15%)
  local copies, waits for them, and re-layouts  137 us (10%)
  blocking collectives  110 us (8%)
  between operations  21.8 us (2%)
    reduce_scatter x4, waiting for transfers between devices, per_device(): lax.psum_scatter(for_sending(placed), ('ctx', 'group'), scatter_dimension...  309 us
    dot_general x4, matrix products, one_block(): jnp.einsum('qhd,khd->hqk', query_blk, keys, preferred_element_type=jnp.fl...  84.3 us
    convert_element_type x2, other arithmetic, one_block(): grad_scores = (probs * (grad_probs - inner)).astype(jnp.bfloat16)  80.9 us
    dot_general x2, matrix products, one_block(): jnp.einsum('qhd,khd->hqk', grad_blk, values, preferred_element_type=jnp.f...  68.5 us
    unnamed x3, blocking collectives  64.8 us
    all_gather x1, waiting for transfers between devices, per_device(): lax.all_gather(shards[13], 'group', axis=0, tiled=True)  60.3 us
    unnamed x229, local copies, waits for them, and re-layouts  46.4 us
    dot_general x2, matrix products, one_block(): jnp.einsum('hqk,qhd->khd', probs.astype(jnp.bfloat16), grad_blk, preferre...  45.3 us
  transfers between devices with their start and end apart: 15, of which 8 were waited for; matrix products, arithmetic and copies ran while one was open for 27% of the time, Pallas kernels for 0%

commit v1 on v0

v1 whole, which is shorter than its diff:
```python
import functools

import jax
import jax.numpy as jnp
from jax import lax
from jax.experimental import pallas as pl
from jax.experimental.pallas import tpu as pltpu
from jax.sharding import PartitionSpec as P

HEADS = 12
HEAD = 64
EPS = 1e-06
BF = jnp.bfloat16
F32 = jnp.float32
NT = (((1,), (1,)), ((), ()))
LOG2E = 1.4426950408889634
LN2 = 0.6931471805599453
SHIFT = 10.0
ALPHA = LOG2E * HEAD ** (-0.5)
AUG = 16
QCH = 3
VMEM = pl.BlockSpec(memory_space=pltpu.VMEM)
SMEM = pl.BlockSpec(memory_space=pltpu.SMEM)
ANY = pl.BlockSpec(memory_space=pl.ANY)


def params(limit=62 * 2**20):
    return pltpu.CompilerParams(vmem_limit_bytes=limit)


def cost(flops, nbytes, trans=0):
    return pl.CostEstimate(flops=int(flops), bytes_accessed=int(nbytes), transcendentals=int(trans))


def dot(a, b):
    return jnp.dot(a, b, preferred_element_type=F32)


def dot_nt(a, b):
    return lax.dot_general(a, b, NT, preferred_element_type=F32)


def rows_norm(x):
    mean = jnp.mean(x, -1, keepdims=True)
    cent = x - mean
    rstd = lax.rsqrt(jnp.mean(cent * cent, -1, keepdims=True) + EPS)
    return cent * rstd, rstd


def rows_norm_back(grad, normed, rstd, gain):
    eg = grad * gain
    return (
        eg - jnp.mean(eg, -1, keepdims=True) - normed * jnp.mean(eg * normed, -1, keepdims=True)
    ) * rstd


def split3(row):
    hi = row.astype(BF)
    rest = row - hi.astype(F32)
    mid = rest.astype(BF)
    low = (rest - mid.astype(F32)).astype(BF)
    return hi.astype(F32), mid.astype(F32), low.astype(F32)


def aug_rows(row):
    hi, mid, low = split3(row)
    at = lax.broadcasted_iota(jnp.int32, (AUG, row.shape[1]), 0)
    out = jnp.where(at == 0, hi, jnp.where(at == 1, mid, jnp.where(at == 2, low, 0.0)))
    return out.astype(BF)


def ones_rows(n):
    at = lax.broadcasted_iota(jnp.int32, (AUG, n), 0)
    return jnp.where(at < 3, 1.0, 0.0).astype(BF)


class Plan:
    def __init__(self, mesh):
        self.X = mesh.shape["ctx"]
        self.G = mesh.shape["group"]
        self.R = mesh.shape["replica"]
        self.Y = self.R // 2
        self.fast = self.X == 2 and self.Y == 2 and (768 // self.G) % 64 == 0
        self.NXY = 4 if self.fast else 1
        self.zrows = 768 // self.G
        self.prow = self.zrows // self.NXY
        ff = 3072 // self.G
        self.NM = 2 if (ff // 2) % 128 == 0 and self.fast else 3
        self.SEG = ff // self.NM
        self.CH = 768 // self.SEG
        self.drow = self.SEG // self.NXY // 2
        self.upc = self.G // 2
        self.uprows = self.upc * self.prow
        self.mrows = self.uprows + self.CH * self.drow

    def perm(self, dx, dy, dc, dz):
        pairs = []
        for x in range(self.X):
            for z in range(self.G):
                for y in range(self.Y):
                    for c in range(2):
                        src = (x * self.G + z) * self.R + 2 * y + c
                        dst = ((x ^ dx) * self.G + (z + dz) % self.G) * self.R + 2 * (y ^ dy) + (c ^ dc)
                        pairs.append((src, dst))
        return pairs

    def send(self, v, dx=0, dy=0, dc=0, dz=0):
        return lax.ppermute(v, ("ctx", "group", "replica"), self.perm(dx, dy, dc, dz))

    def swap(self, v):
        pairs = []
        for z in range(self.G):
            for y in range(self.Y):
                a = z * self.R + 2 * y + 1
                b = (self.G + z) * self.R + 2 * y
                pairs += [(a, b), (b, a)]
        return lax.ppermute(v, ("ctx", "group", "replica"), pairs)


PLANE = ((0, 0), (0, 1), (1, 0), (1, 1))


def norm_in_kernel(own_ref, oth_ref, vec_ref, h_ref):
    gain, shift = vec_ref[0:1, :], vec_ref[1:2, :]
    rows = own_ref.shape[0]
    n, _ = rows_norm(own_ref[...].astype(F32))
    h_ref[pl.ds(0, rows), :] = (n * gain + shift).astype(BF)
    n, _ = rows_norm(oth_ref[...].astype(F32))
    h_ref[pl.ds(rows, rows), :] = (n * gain + shift).astype(BF)


def norm_in(own, oth, vec):
    rows, width = own.shape
    return pl.pallas_call(
        norm_in_kernel,
        in_specs=[VMEM] * 3,
        out_specs=VMEM,
        out_shape=jax.ShapeDtypeStruct((2 * rows, width), BF),
        compiler_params=params(),
        cost_estimate=cost(20 * 2 * rows * width, 8 * rows * width),
    )(own, oth, vec)


def load_rows(plan, sc_ref, stacks, dst_of, sem):
    copies = []
    for e, d, ref in stacks:
        for s in range(plan.G):
            copies += [
                pltpu.make_async_copy(src, dst, sem) for src, dst in dst_of(e, d, s, ref)
            ]
    for c in copies:
        c.start()
    return copies


def piece_at(plan, sc_ref, d, s, sign):
    xy = sc_ref[2] ^ d if plan.NXY > 1 else 0
    z = lax.rem(sc_ref[3] + (plan.G - s if sign < 0 else s), plan.G)
    return xy, z


def fwd_kernel(plan, chunk, sc_ref, h_ref, bias_ref, gains_ref, *refs):
    stacks = refs[: plan.NXY]
    q_out, k_out, v_out, nq_out, nk_out, r_out, own_out, oth_out, lo_out, w_ref = refs[plan.NXY : plan.NXY + 10]
    kn_ref, acc_ref, sem = refs[plan.NXY + 10 :]
    rows = h_ref.shape[0]

    def dst_of(e, d, s, ref):
        xy, z = piece_at(plan, sc_ref, d, s, -1)
        at = pl.multiple_of(z * plan.zrows + xy * plan.prow, 16)
        return [(ref.at[s], w_ref.at[pl.ds(at, plan.prow), :])]

    copies = load_rows(plan, sc_ref, [(0, d, stacks[d]) for d in range(plan.NXY)], dst_of, sem)
    for c in copies:
        c.wait()
    wt = w_ref[...].T
    ones = ones_rows(rows)
    at = lax.broadcasted_iota(jnp.int32, (AUG, rows), 0)
    minus = jnp.where(at == 0, -SHIFT, 0.0).astype(BF)
    for part in range(3):
        y = dot_nt(wt[128 * part : 128 * part + 128, :], h_ref[...])
        y = y + bias_ref[128 * part : 128 * part + 128, chunk : chunk + 1]
        for a in range(2):
            x = y[64 * a : 64 * a + 64, :]
            if part == 2:
                v_out[a, 0:64, :] = x.astype(BF)
                v_out[a, 64:80, :] = ones
                continue
            mean = jnp.mean(x, 0, keepdims=True)
            cent = x - mean
            rstd = lax.rsqrt(jnp.mean(cent * cent, 0, keepdims=True) + EPS)
            n = cent * rstd
            r_out[2 * part + a : 2 * part + a + 1, :] = rstd
            if part == 0:
                nq_out[64 * a : 64 * a + 64, :] = n.astype(BF)
                val = (n * gains_ref[:, 0:1] + gains_ref[:, 1:2]) * ALPHA
                q_out[a, 0:64, :] = val.astype(BF)
                q_out[a, 64:80, :] = minus
            else:
                nk_out[64 * a : 64 * a + 64, :] = n.astype(BF)
                k_out[a, 0:64, :] = (n * gains_ref[:, 2:3]).astype(BF)
                k_out[a, 64:80, :] = ones

    kb = 512
    half = rows // 2

    def head(a, _):
        kn_ref[...] = k_out[a].T
        acc = None
        for j in range(rows // kb):
            st = dot(kn_ref[j * kb : (j + 1) * kb, :], q_out[a])
            p = jnp.exp2(st).astype(BF)
            o = dot(v_out[a, :, j * kb : (j + 1) * kb], p)
            if j == 0:
                acc_ref[...] = o
            else:
                acc_ref[...] += o
        total = acc_ref[64:65, :]
        inv = 1.0 / total
        full = acc_ref[0:64, :] * inv
        o = full.astype(BF)
        at0 = pl.multiple_of(a * 64, 64)
        own_out[pl.ds(at0, 64), :] = o[:, :half]
        oth_out[pl.ds(at0, 64), :] = o[:, half:]
        lo_out[pl.ds(at0, 64), :] = (full - o.astype(F32)).astype(BF)
        q_out[a, 64:80, :] = aug_rows(-(SHIFT + jnp.log(total) * LOG2E))
        return 0

    lax.fori_loop(0, 2, head, 0)


def attend_fwd(plan, chunk, sc, h1, bias, gains, stacks):
    rows = h1.shape[0]
    sd = jax.ShapeDtypeStruct
    return pl.pallas_call(
        functools.partial(fwd_kernel, plan, chunk),
        in_specs=[SMEM, VMEM, VMEM, VMEM] + [ANY] * plan.NXY,
        out_specs=[VMEM] * 10,
        out_shape=[
            sd((2, 80, rows), BF),
            sd((2, 80, rows), BF),
            sd((2, 80, rows), BF),
            sd((128, rows), BF),
            sd((128, rows), BF),
            sd((8, rows), F32),
            sd((128, rows // 2), BF),
            sd((128, rows // 2), BF),
            sd((128, rows), BF),
            sd((768, 384), BF),
        ],
        scratch_shapes=[
            pltpu.VMEM((rows, 80), BF),
            pltpu.VMEM((80, rows), F32),
            pltpu.SemaphoreType.DMA,
        ],
        compiler_params=params(),
        cost_estimate=cost(16e9, 10e6, 8.4e6),
    )(sc, h1, bias, gains, *stacks)


def out_kernel(plan, sc_ref, pat_ref, vec_ref, *refs):
    at_refs = refs[:6]
    stacks = refs[6 : 6 + 2 * plan.NXY]
    x1_out, h2_out, w_ref = refs[6 + 2 * plan.NXY : 9 + 2 * plan.NXY]
    an_ref, sem = refs[9 + 2 * plan.NXY :]

    def dst_of(e, d, s, ref):
        xy, z = piece_at(plan, sc_ref, d, s, -1)
        at = pl.multiple_of(z * plan.zrows + xy * plan.prow, 16)
        return [(ref.at[s], w_ref.at[sc_ref[1] ^ e, pl.ds(at, plan.prow), :])]

    copies = load_rows(
        plan,
        sc_ref,
        [(e, d, stacks[e * plan.NXY + d]) for e in range(2) for d in range(plan.NXY)],
        dst_of,
        sem,
    )
    for m in range(6):
        off = (sc_ref[0] if m < 3 else 1 - sc_ref[0]) * 384 + (m % 3) * 128
        an_ref[:, pl.ds(pl.multiple_of(off, 128), 128)] = at_refs[m][...].T
    for c in copies:
        c.wait()
    for i in range(2):
        x1_out[:, 384 * i : 384 * i + 384] = (
            dot(an_ref[...], w_ref[i])
            + pat_ref[:, 384 * i : 384 * i + 384].astype(F32)
            + vec_ref[2:3, 384 * i : 384 * i + 384]
        )
    n, _ = rows_norm(x1_out[...])
    h2_out[...] = (n * vec_ref[3:4, :] + vec_ref[4:5, :]).astype(BF)


def out_proj(plan, sc, pat, vec, attn, stacks):
    rows, width = pat.shape
    sd = jax.ShapeDtypeStruct
    return pl.pallas_call(
        functools.partial(out_kernel, plan),
        in_specs=[SMEM, VMEM, VMEM] + [VMEM] * 6 + [ANY] * (2 * plan.NXY),
        out_specs=[VMEM] * 3,
        out_shape=[sd((rows, width), F32), sd((rows, width), BF), sd((2, 768, 384), BF)],
        scratch_shapes=[pltpu.VMEM((rows, 768), BF), pltpu.SemaphoreType.DMA],
        compiler_params=params(),
        cost_estimate=cost(2 * rows * 768 * 768, 12e6),
    )(sc, pat, vec, *attn, *stacks)


def gelu_parts(value):
    coeff = (2.0 / jnp.pi) ** 0.5
    sq = value * value
    tangent = jnp.tanh(coeff * value * (1.0 + 0.044715 * sq))
    half = 0.5 * (1.0 + tangent)
    slope = half + 0.5 * value * (1.0 - tangent * tangent) * (coeff * (1.0 + 3.0 * 0.044715 * sq))
    return value * half, slope


def mlp_kernel(plan, last, sc_ref, h_ref, g_ref, y_in, dh_in, bup_ref, vec_ref, *refs):
    stacks = refs[: 2 * plan.NXY]
    y_out, dh_out, sb_out, keep_ref, send_ref = refs[2 * plan.NXY : 2 * plan.NXY + 5]
    wu_ref, wd_ref, gu_ref, gd_ref, ht_ref, acc_ref, sem = refs[2 * plan.NXY + 5 :]
    G, SEG, CH = plan.G, plan.SEG, plan.CH

    def spots(e, d, s, ref, sign, up, down, c_at):
        xy, z = piece_at(plan, sc_ref, d, s, sign)
        cc = sc_ref[1] ^ e
        a0 = pl.multiple_of(z * plan.zrows + xy * plan.prow, 16)
        b0 = pl.multiple_of(z * SEG + (xy * 2 + cc) * plan.drow, 16)
        if plan.fast:
            yield up.at[pl.ds(cc * plan.upc, plan.upc), pl.ds(a0, plan.prow), :], slice(0, plan.upc)
            yield down.at[:, pl.ds(b0, plan.drow), :], slice(plan.upc, 2 * plan.upc)
            return
        for u in range(plan.upc):
            yield up.at[cc * plan.upc + u, pl.ds(a0, plan.prow), :], pl.ds(u * plan.prow, plan.prow)
        for v in range(CH):
            yield down.at[v, pl.ds(b0, plan.drow), :], pl.ds(plan.uprows + v * plan.drow, plan.drow)

    copies = []
    for e in range(2):
        for d in range(plan.NXY):
            ref = stacks[e * plan.NXY + d]
            for s in range(G):
                for spot, at in spots(e, d, s, ref, -1, wu_ref, wd_ref, None):
                    copies.append(pltpu.make_async_copy(ref.at[s, at], spot, sem))
    for c in copies:
        c.start()
    ht_ref[...] = h_ref[...].T
    for c in copies:
        c.wait()

    def seg(f, _):
        fs = pl.ds(pl.multiple_of(f * SEG, 128), SEG)
        u = dot(h_ref[...], wu_ref[f]) + bup_ref[pl.ds(f, 1), :]
        z, slope = gelu_parts(u)
        zb = z.astype(BF)
        dz = jnp.zeros(u.shape, F32)
        for v in range(CH):
            wd = wd_ref[v, fs, :]
            cs = slice(v * SEG, (v + 1) * SEG)
            dz = dz + dot_nt(g_ref[:, cs], wd)
            upd = dot(zb, wd)
            acc_ref[:, cs] += upd
        du = (dz * slope).astype(BF)
        zt = zb.T
        for v in range(CH):
            cs = slice(v * SEG, (v + 1) * SEG)
            gd_ref[v, fs, :] = dot(zt, g_ref[:, cs]).astype(BF)
        gu_ref[f] = dot(ht_ref[...], du).astype(BF)
        dh_out[...] += dot_nt(du, wu_ref[f])
        sb_out[pl.ds(f, 1), :] = jnp.sum(du.astype(F32), 0, keepdims=True)
        return 0

    acc_ref[...] = y_in[...]
    if dh_in is None:
        dh_out[...] = jnp.zeros(dh_out.shape, F32)
    else:
        dh_out[...] = dh_in[...]
    lax.fori_loop(0, G, seg, 0)
    outs = []
    for e in (1, 0):
        dst = send_ref if e else keep_ref
        for d in range(plan.NXY):
            for s in range(G):
                for spot, at in spots(e, d, s, None, 1, gu_ref, gd_ref, None):
                    outs.append(pltpu.make_async_copy(spot, dst.at[d, s, at], sem))
    for c in outs:
        c.start()
    if last:
        y_out[...] = (acc_ref[...] + vec_ref[5:6, :]).astype(BF)
    else:
        y_out[...] = acc_ref[...]
    for c in outs:
        c.wait()


def mlp_part(plan, last, sc, h2, g, y, dh, bup, vec, stacks):
    rows, width = h2.shape
    sd = jax.ShapeDtypeStruct
    first = dh is None

    def body(sc_ref, h_ref, g_ref, y_in, *rest):
        if first:
            return mlp_kernel(plan, last, sc_ref, h_ref, g_ref, y_in, None, *rest)
        return mlp_kernel(plan, last, sc_ref, h_ref, g_ref, y_in, *rest)

    piece = (2 * plan.upc, plan.prow, plan.SEG) if plan.fast else (plan.mrows, plan.SEG)
    ga = sd((plan.NXY, plan.G) + piece, BF)
    ffp = 3072 // plan.NM
    return pl.pallas_call(
        body,
        in_specs=[SMEM, VMEM, VMEM, VMEM] + ([] if first else [VMEM]) + [VMEM, VMEM] + [ANY] * (2 * plan.NXY),
        out_specs=[VMEM, VMEM, VMEM, ANY, ANY],
        out_shape=[
            sd((rows, width), BF if last else F32),
            sd((rows, width), F32),
            sd((plan.G, plan.SEG), F32),
            ga,
            ga,
        ],
        scratch_shapes=[
            pltpu.VMEM((plan.G, 768, plan.SEG), BF),
            pltpu.VMEM((plan.CH, ffp, plan.SEG), BF),
            pltpu.VMEM((plan.G, 768, plan.SEG), BF),
            pltpu.VMEM((plan.CH, ffp, plan.SEG), BF),
            pltpu.VMEM((768, rows), BF),
            pltpu.VMEM((rows, width), F32),
            pltpu.SemaphoreType.DMA,
        ],
        compiler_params=params(),
        cost_estimate=cost(12 * rows * 768 * ffp, 24e6, rows * ffp),
    )(sc, h2, g, y, *([] if first else [dh]), bup, vec, *stacks)


def mid_back_kernel(plan, sc_ref, x1_ref, dh_ref, g_ref, vec_ref, w_ref, *refs):
    at_refs = refs[:6]
    dx_out, sv_out, keep_ref, send_ref = refs[6:10]
    da_outs = refs[10:16]
    gw_ref, sem = refs[16:]
    dh = dh_ref[...]
    n, rstd = rows_norm(x1_ref[...])
    g = g_ref[...].astype(F32)
    dx = g + rows_norm_back(dh, n, rstd, vec_ref[3:4, :])
    dx_out[...] = dx
    da = dx.astype(BF)
    sv_out[...] = jnp.zeros(sv_out.shape, F32)
    sv_out[0:1, :] = jnp.sum(da.astype(F32), 0, keepdims=True)
    sv_out[1:2, :] = jnp.sum(dh * n, 0, keepdims=True)
    sv_out[2:3, :] = jnp.sum(dh, 0, keepdims=True)
    sv_out[3:4, :] = jnp.sum(g, 0, keepdims=True)
    for m in range(6):
        off = (sc_ref[0] if m < 3 else 1 - sc_ref[0]) * 384 + (m % 3) * 128
        rs = pl.ds(pl.multiple_of(off, 128), 128)
        da_outs[m][...] = (
            dot_nt(w_ref[0, rs, :], da[:, :384]) + dot_nt(w_ref[1, rs, :], da[:, 384:])
        ).astype(BF)
        for i in range(2):
            gw_ref[i, rs, :] = dot(at_refs[m][...], da[:, 384 * i : 384 * i + 384]).astype(BF)
    outs = []
    for e in (1, 0):
        dst = send_ref if e else keep_ref
        for d in range(plan.NXY):
            for s in range(plan.G):
                xy, z = piece_at(plan, sc_ref, d, s, 1)
                at = pl.multiple_of(z * plan.zrows + xy * plan.prow, 16)
                outs.append(
                    pltpu.make_async_copy(
                        gw_ref.at[sc_ref[1] ^ e, pl.ds(at, plan.prow), :], dst.at[d, s], sem
                    )
                )
    for c in outs:
        c.start()
    for c in outs:
        c.wait()


def mid_back(plan, sc, x1, dh2, g, vec, wout, attn):
    rows, width = x1.shape
    sd = jax.ShapeDtypeStruct
    ga = sd((plan.NXY, plan.G, plan.prow, 384), BF)
    return pl.pallas_call(
        functools.partial(mid_back_kernel, plan),
        in_specs=[SMEM] + [VMEM] * 5 + [VMEM] * 6,
        out_specs=[VMEM, VMEM, ANY, ANY] + [VMEM] * 6,
        out_shape=[sd((rows, width), F32), sd((8, width), F32), ga, ga] + [sd((128, rows), BF)] * 6,
        scratch_shapes=[pltpu.VMEM((2, 768, 384), BF), pltpu.SemaphoreType.DMA],
        compiler_params=params(),
        cost_estimate=cost(4 * rows * 768 * 768, 20e6),
    )(sc, x1, dh2, g, vec, wout, *attn)


def bwd_kernel(plan, sc_ref, h_ref, q_ref, k_ref, v_ref, nq_ref, nk_ref, r_ref, own_ref, oth_ref, lo_ref, do_own, do_oth, gains_ref, *refs):
    dqkv_out, ga_ref, sb_out, sg_out = refs[:4]
    qn_ref, kn_ref, dn_ref, dt_ref, dq_ref, dk_ref, dv_ref, gw_ref, sem = refs[4:]
    rows = h_ref.shape[0]
    half = rows // 2
    qb = kb = 512
    sg_out[...] = jnp.zeros(sg_out.shape, F32)

    def head(a, _):
        at0 = pl.ds(pl.multiple_of(a * 64, 64), 64)
        for t, (o_ref, d_ref) in enumerate(((own_ref, do_own), (oth_ref, do_oth))):
            ls = slice(t * half, (t + 1) * half)
            do = d_ref[at0, :]
            o = o_ref[at0, :].astype(F32) + lo_ref[at0, ls].astype(F32)
            dsum = jnp.sum(do.astype(F32) * o, 0, keepdims=True)
            dt_ref[0:64, ls] = do
            dt_ref[64:80, ls] = aug_rows(-dsum)
        qn_ref[...] = q_ref[a].T
        kn_ref[...] = k_ref[a].T
        dn_ref[...] = dt_ref[...].T

        for i in range(rows // qb):
            rs = slice(i * qb, (i + 1) * qb)
            dq = None
            for j in range(rows // kb):
                ks = slice(j * kb, (j + 1) * kb)
                p = jnp.exp2(dot(qn_ref[rs, :], k_ref[a, :, ks]))
                dp = dot(dn_ref[rs, :], v_ref[a, :, ks])
                ds = (p * dp).astype(BF)
                t = dot(ds, kn_ref[ks, :])
                dq = t if dq is None else dq + t
                tv = dot(dt_ref[0:64, rs], p.astype(BF))
                tk = dot(q_ref[a, 0:64, rs], ds)
                if i == 0:
                    dv_ref[:, ks] = tv
                    dk_ref[:, ks] = tk
                else:
                    dv_ref[:, ks] += tv
                    dk_ref[:, ks] += tk
            dq_ref[:, rs] = dq.T[:64]

        def norm_back(e, n, rstd, gain):
            eg = e * gain
            return rstd * (
                eg - jnp.mean(eg, 0, keepdims=True) - n * jnp.mean(eg * n, 0, keepdims=True)
            )

        e = dq_ref[...] * HEAD ** (-0.5)
        n = nq_ref[at0, :].astype(F32)
        dqkv_out[at0, :] = norm_back(e, n, r_ref[pl.ds(a, 1), :], gains_ref[:, 0:1]).astype(BF)
        sg_out[:, 0:1] += jnp.sum(e * n, 1, keepdims=True)
        sg_out[:, 1:2] += jnp.sum(e, 1, keepdims=True)
        e = dk_ref[...] * LN2
        n = nk_ref[at0, :].astype(F32)
        dqkv_out[pl.ds(pl.multiple_of(128 + a * 64, 64), 64), :] = norm_back(
            e, n, r_ref[pl.ds(2 + a, 1), :], gains_ref[:, 2:3]
        ).astype(BF)
        sg_out[:, 2:3] += jnp.sum(e * n, 1, keepdims=True)
        dqkv_out[pl.ds(pl.multiple_of(256 + a * 64, 64), 64), :] = dv_ref[...].astype(BF)
        return 0

    lax.fori_loop(0, 2, head, 0)
    gw_ref[...] = dot(dqkv_out[...], h_ref[...]).T.astype(BF)
    outs = []
    for d in range(plan.NXY):
        for s in range(plan.G):
            xy, z = piece_at(plan, sc_ref, d, s, 1)
            at = pl.multiple_of(z * plan.zrows + xy * plan.prow, 16)
            outs.append(
                pltpu.make_async_copy(gw_ref.at[pl.ds(at, plan.prow), :], ga_ref.at[d, s], sem)
            )
    for c in outs:
        c.start()
    sb_out[...] = jnp.broadcast_to(
        jnp.sum(dqkv_out[...].astype(F32), 1, keepdims=True), sb_out.shape
    )
    for c in outs:
        c.wait()


def attend_bwd(plan, sc, h1, saved, do_own, do_oth, gains):
    rows = h1.shape[0]
    sd = jax.ShapeDtypeStruct
    return pl.pallas_call(
        functools.partial(bwd_kernel, plan),
        in_specs=[SMEM] + [VMEM] * 13,
        out_specs=[VMEM, ANY, VMEM, VMEM],
        out_shape=[
            sd((384, rows), BF),
            sd((plan.NXY, plan.G, plan.prow, 384), BF),
            sd((384, 128), F32),
            sd((64, 128), F32),
        ],
        scratch_shapes=[
            pltpu.VMEM((rows, 80), BF),
            pltpu.VMEM((rows, 80), BF),
            pltpu.VMEM((rows, 80), BF),
            pltpu.VMEM((80, rows), BF),
            pltpu.VMEM((64, rows), F32),
            pltpu.VMEM((64, rows), F32),
            pltpu.VMEM((64, rows), F32),
            pltpu.VMEM((768, 384), BF),
            pltpu.SemaphoreType.DMA,
        ],
        compiler_params=params(),
        cost_estimate=cost(40e9, 12e6, 8.4e6),
    )(sc, h1, *saved, do_own, do_oth, gains)


def dh_oth_kernel(*refs):
    dq, w, out_ref = refs[:QCH], refs[QCH : 2 * QCH], refs[-1]
    half = out_ref.shape[0]
    acc = None
    for j in range(QCH):
        t = dot_nt(dq[j][:, half:].T, w[j][...])
        acc = t if acc is None else acc + t
    out_ref[...] = acc.astype(BF)


def dh_oth(dqkv, w):
    rows = dqkv[0].shape[1]
    return pl.pallas_call(
        dh_oth_kernel,
        in_specs=[VMEM] * (2 * QCH),
        out_specs=VMEM,
        out_shape=jax.ShapeDtypeStruct((rows // 2, 768), BF),
        compiler_params=params(),
        cost_estimate=cost(rows * 768 * 1152, 8e6),
    )(*dqkv, *w)


def dh_own_kernel(rcv_ref, pat_ref, dx_ref, vec_ref, *refs):
    dq, w = refs[:QCH], refs[QCH : 2 * QCH]
    out_ref, low_ref, sv_out = refs[2 * QCH :]
    half = out_ref.shape[0]
    dh = rcv_ref[...].astype(F32)
    for j in range(QCH):
        dh = dh + dot_nt(dq[j][:, :half].T, w[j][...])
    n, rstd = rows_norm(pat_ref[...].astype(F32))
    out = dx_ref[...] + rows_norm_back(dh, n, rstd, vec_ref[0:1, :])
    out_ref[...] = out
    low_ref[...] = out.astype(BF)
    sv_out[...] = jnp.zeros(sv_out.shape, F32)
    sv_out[0:1, :] = jnp.sum(dh * n, 0, keepdims=True)
    sv_out[1:2, :] = jnp.sum(dh, 0, keepdims=True)


def dh_own(rcv, pat, dx, vec, dqkv, w):
    rows, width = pat.shape
    sd = jax.ShapeDtypeStruct
    return pl.pallas_call(
        dh_own_kernel,
        in_specs=[VMEM] * (4 + 2 * QCH),
        out_specs=[VMEM] * 3,
        out_shape=[sd((rows, width), F32), sd((rows, width), BF), sd((8, width), F32)],
        compiler_params=params(),
        cost_estimate=cost(2 * rows * 768 * 1152, 20e6),
    )(rcv, pat, dx, vec, *dqkv, *w)


def add_kernel(n, *refs):
    ins, outs = refs[:n], refs[n:]
    for k, out in enumerate(outs):
        acc = ins[0][k].astype(F32)
        for r in ins[1:]:
            acc = acc + r[k].astype(F32)
        out[...] = acc.astype(out.dtype)


def add_split(arrays):
    shape = arrays[0].shape
    n = len(arrays)
    size = 2 * arrays[0].size
    return pl.pallas_call(
        functools.partial(add_kernel, n),
        in_specs=[VMEM] * n,
        out_specs=[VMEM] * shape[0],
        out_shape=[jax.ShapeDtypeStruct(shape[1:], BF)] * shape[0],
        compiler_params=params(),
        cost_estimate=cost(n * arrays[0].size, (n + 1) * size),
    )(*arrays)


def gather_pieces(plan, piece, cores):
    if not plan.fast:
        both = piece if cores else piece[None]
        every = lax.all_gather(both, "group", axis=0)
        every = jnp.stack([every[(-s) % plan.G] for s in range(plan.G)])
        return [every[:, i] for i in range(both.shape[0])]
    got = [piece] + [plan.send(piece, dz=s) for s in range(1, plan.G)]
    stack = jnp.stack(got)
    plane = [stack] + [plan.send(stack, dx=dx, dy=dy) for dx, dy in PLANE[1:]]
    if cores:
        plane = plane + [plan.send(v, dc=1) for v in plane]
    return plane


def reduce_pieces(plan, keep, send):
    cores = send is not None
    if not plan.fast:
        if cores:
            both = jnp.stack([keep[0], send[0]])
        else:
            c = lax.axis_index("replica") % 2
            zero = jnp.zeros_like(keep[0])
            both = jnp.where(c == 0, jnp.stack([keep[0], zero]), jnp.stack([zero, keep[0]]))
        mine = lax.psum_scatter(both, "group", scatter_dimension=1, tiled=True)
        mine = lax.psum(mine, ("ctx", "replica"))
        return [mine[0, 0], mine[1, 0]]
    if cores:
        parts = add_split([keep, plan.send(send, dc=1)])
    else:
        parts = [keep[i] for i in range(4)]
    arrived = [parts[0]] + [plan.send(parts[i], dx=dx, dy=dy) for i, (dx, dy) in enumerate(PLANE) if i]
    parts = add_split(arrived)
    arrived = [parts[0]] + [plan.send(parts[s], dz=s) for s in range(1, plan.G)]
    total = add_split([a[None] for a in arrived])[0]
    plane = [total] + [plan.send(total, dx=dx, dy=dy) for dx, dy in PLANE[1:]]
    return plane + [plan.send(v, dc=1) for v in plane]


def per_device(plan, *args):
    (
        patches, cotangent, wqkv, bqkv, qgain, qshift, kgain, gain1, shift1, wout, bout,
        gain2, shift2, wup, bup, wdown, bdown,
    ) = args
    G, SEG, NM, NXY = plan.G, plan.SEG, plan.NM, plan.NXY
    images, local, width = patches.shape
    x = lax.axis_index("ctx")
    z = lax.axis_index("group")
    r = lax.axis_index("replica")
    y, c = r // 2, r % 2
    zero = jnp.zeros((), jnp.int32)
    fast = plan.fast
    sc = jnp.stack([c, c if fast else zero, 2 * x + y if fast else zero, z if fast else zero]).astype(jnp.int32)
    stay = x == c

    pat0 = patches.reshape(local, width)
    cot0 = cotangent.reshape(local, width)
    pat = jnp.where(stay, pat0, plan.swap(pat0))
    pat_oth = plan.send(pat, dc=1)

    small = jnp.concatenate(
        [
            jnp.stack([gain1, shift1, bout, gain2, shift2, bdown]).reshape(-1),
            bup.reshape(-1),
            bqkv.reshape(-1),
            qgain,
            qshift,
            kgain,
        ]
    )
    got = [small] + [plan.send(small, dz=s) for s in range(1, G)]
    stackd = jnp.stack(got)
    every = jnp.take(stackd, (z - jnp.arange(G)) % G, axis=0).astype(F32)
    zr = plan.zrows
    vec = every[:, : 6 * zr].reshape(G, 6, zr).transpose(1, 0, 2).reshape(6, 768)
    vec = jnp.concatenate([vec, jnp.zeros((2, 768), F32)])
    at = 6 * zr
    ffz = 3072 // G
    bup_all = every[:, at : at + ffz].reshape(G, NM, SEG)
    at += ffz
    bq_all = every[:, at : at + 3 * zr].reshape(3, 2, QCH, 128)
    at += 3 * zr
    bias = lax.dynamic_index_in_dim(bq_all, c, 1, False).transpose(0, 2, 1).reshape(384, QCH)
    bias = jnp.pad(bias, ((0, 0), (0, 128 - QCH)))
    gains = every[:, at:].reshape(G, 3, HEAD // G).transpose(0, 2, 1).reshape(HEAD, 3)
    gains = jnp.pad(gains, ((0, 0), (0, 125)))

    pr = plan.prow
    xy = sc[2]

    def rows_of(v, n):
        return lax.dynamic_slice_in_dim(v, xy * n, n, 0)

    wq = rows_of(wqkv, pr).reshape(pr, 3, 2, QCH, 128)
    wq = lax.dynamic_index_in_dim(wq, c, 2, False)
    qpieces = [wq[:, :, j].reshape(pr, 384) for j in range(QCH)]
    qst = [gather_pieces(plan, p, False) for p in qpieces]

    wo = rows_of(wout, pr).reshape(pr, 2, 384).transpose(1, 0, 2)
    wu = rows_of(wup, pr).reshape(pr, G, NM, SEG)
    wd = wdown.reshape(NM, NXY, 2, plan.drow, plan.CH, SEG)
    wd = lax.dynamic_index_in_dim(wd, xy, 1, False)

    def own_core(v):
        return lax.dynamic_index_in_dim(v, c, 0, False) if fast else v

    wo = own_core(wo)

    def mpiece(t):
        up = wu[:, :, t].reshape(pr, 2, plan.upc, SEG).transpose(1, 2, 0, 3)
        down = wd[t].transpose(0, 2, 1, 3)
        if not fast:
            up, down = up.reshape(2, -1, SEG), down.reshape(2, -1, SEG)
        return own_core(jnp.concatenate([up, down], 1))

    mpieces = [mpiece(t) for t in range(NM)]
    ost = gather_pieces(plan, wo, True)
    mst = [gather_pieces(plan, p, True) for p in mpieces]

    cot = jnp.where(stay, cot0, plan.swap(cot0))

    h1 = norm_in(pat, pat_oth, vec)
    saved, own_o, oth_o, wqs = [], [], [], []
    for j in range(QCH):
        *keep, own, oth, low, w = attend_fwd(plan, j, sc, h1, bias, gains, qst[j])
        saved.append((*keep, own, oth, low))
        own_o.append(own)
        oth_o.append(plan.send(oth, dc=1))
        wqs.append(w)
    attn = own_o + oth_o
    x1, h2, wo_full = out_proj(plan, sc, pat, vec, attn, ost)
    yv, dh2 = x1, None
    sbs, mgrads = [], []
    for t in range(NM):
        yv, dh2, sb, keep, send = mlp_part(
            plan, t == NM - 1, sc, h2, cot, yv, dh2, bup_all[:, t], vec, mst[t]
        )
        sbs.append(sb)
        mgrads.append(reduce_pieces(plan, keep, send))
    layer_out = jnp.where(stay, yv, plan.swap(yv))

    dx1, sv3, okeep, osend, *dattn = mid_back(plan, sc, x1, dh2, cot, vec, wo_full, attn)
    ograd = reduce_pieces(plan, okeep, osend)
    dqkv, qgrads, sbq, sgq = [], [], [], []
    for j in range(QCH):
        far = plan.send(dattn[QCH + j], dc=1)
        d, ga, sb, sg = attend_bwd(plan, sc, h1, saved[j], dattn[j], far, gains)
        dqkv.append(d)
        qgrads.append(reduce_pieces(plan, ga, None))
        sbq.append(sb)
        sgq.append(sg)
    rcv = plan.send(dh_oth(dqkv, wqs), dc=1)
    gp, gp_low, sv1 = dh_own(rcv, pat, dx1, vec, dqkv, wqs)
    grad_patches = jnp.where(stay, gp, plan.swap(gp_low).astype(F32))

    def place(pieces, rows):
        if not fast:
            return jnp.stack([p[None] for p in pieces])
        st = jnp.stack(pieces).reshape((2, 4) + pieces[0].shape)
        order = xy ^ jnp.arange(4)
        st = jnp.take(st, order, axis=1)
        return jnp.where(c == 0, st, st[::-1])

    og = place(ograd, pr)
    g_wout = og.transpose(1, 2, 0, 3).reshape(zr, 768).astype(F32)
    ups, downs = [], []
    for t in range(NM):
        mg = place(mgrads[t], pr)
        if not fast:
            mg = mg.reshape(2, NXY, -1, pr, SEG)
        ups.append(mg[:, :, : plan.upc].transpose(1, 3, 0, 2, 4).reshape(zr, G, SEG))
        dn = mg[:, :, plan.upc :].reshape(2, NXY, plan.CH, plan.drow, SEG)
        downs.append(dn.transpose(1, 0, 3, 2, 4).reshape(SEG, 768))
    g_wup = jnp.stack(ups, 2).reshape(zr, 3072).astype(F32)
    g_wdown = jnp.concatenate(downs, 0).astype(F32)
    qg = jnp.stack([place(qgrads[j], pr) for j in range(QCH)])
    g_wqkv = qg.reshape(QCH, 2, zr, 3, 128).transpose(2, 3, 1, 0, 4).reshape(zr, 2304).astype(F32)

    bq = jnp.stack([s[:, 0] for s in sbq])
    bq = bq.reshape(QCH, 3, 128).transpose(1, 0, 2)
    zq = jnp.zeros_like(bq)
    bq = jnp.where(c == 0, jnp.stack([bq, zq], 1), jnp.stack([zq, bq], 1)).reshape(2304)
    sg = sgq[0][:, :3] + sgq[1][:, :3] + sgq[2][:, :3]
    sb = jnp.stack(sbs, 1).reshape(3072)
    v6 = jnp.concatenate([sv1[:2], sv3[:4]])
    pack = jnp.concatenate(
        [
            v6.reshape(6, G, zr).transpose(1, 0, 2).reshape(G, -1),
            sb.reshape(G, -1),
            bq.reshape(G, -1),
            sg.reshape(G, HEAD // G, 3).transpose(0, 2, 1).reshape(G, -1),
        ],
        1,
    )
    total = pack
    if fast:
        rest = [plan.send(pack, dx=dx, dy=dy, dc=dc) for dx, dy in PLANE for dc in range(2) if dx or dy or dc]
        for v in rest:
            total = total + v
        mine = lax.dynamic_index_in_dim(total, z, 0, False)
        for s in range(1, G):
            v = lax.dynamic_index_in_dim(total, (z + s) % G, 0, False)
            mine = mine + plan.send(v, dz=s)
    else:
        mine = lax.psum(total, ("ctx", "replica"))
        mine = lax.psum_scatter(mine, "group", scatter_dimension=0, tiled=True)[0]
    s6 = mine[: 6 * zr].reshape(6, zr)
    at = 6 * zr
    g_bup = mine[at : at + ffz]
    at += ffz
    g_bqkv = mine[at : at + 3 * zr]
    at += 3 * zr
    qk = mine[at:].reshape(3, HEAD // G)
    return (
        layer_out.reshape(images, local, width),
        grad_patches.reshape(images, local, width),
        g_wqkv,
        g_bqkv,
        qk[0],
        qk[1],
        qk[2],
        s6[0],
        s6[1],
        g_wout,
        s6[2],
        s6[3],
        s6[4],
        g_wup,
        g_bup,
        g_wdown,
        s6[5],
    )


def solution(mesh):
    plan = Plan(mesh)
    rows = P(("group", "replica"), "ctx", None)
    mat, vec = P("group", None), P("group")
    weights = (mat, vec, vec, vec, vec, vec, vec, mat, vec, vec, vec, mat, vec, mat, vec)
    return jax.shard_map(
        functools.partial(per_device, plan),
        mesh=mesh,
        in_specs=(rows, rows) + weights,
        out_specs=(rows, rows) + weights,
        check_vma=False,
    )
```

time: 1360 us -> 678 us (0.50)
  matrix products: 388 us -> 0 us
  waiting for transfers between devices: 485 us -> 137 us
  Pallas kernels: 0 us -> 277 us
  other arithmetic: 207 us -> 21.9 us
  starting transfers between devices: 0.6 us -> 163 us
  blocking collectives: 110 us -> 0 us
  local copies, waits for them, and re-layouts: 137 us -> 67.1 us
  between operations: 21.8 us -> 2.57 us
    dot_general x26 -> x0, matrix products: 388 us -> none  [the longest x4 84.3 us: one_block(): jnp.einsum('qhd,khd->hqk', query_blk, keys, preferred_element_type=jnp.fl...]
    reduce_scatter x6 -> x0, waiting for transfers between devices: 309 us -> none  [the longest x4 309 us: per_device(): lax.psum_scatter(for_sending(placed), ('ctx', 'group'), scatter_dimension...]
    pallas_call x0 -> x28, Pallas kernels: none -> 277 us  [the longest x3 84.2 us: attend_bwd(): pl.pallas_call(functools.partial(bwd_kernel, plan), in_specs=[SMEM] + [VM...]
    ppermute x0 -> x154, starting transfers between devices: none -> 163 us  [the longest x150 155 us: send(): lax.ppermute(v, ('ctx', 'group', 'replica'), self.perm(dx, dy, dc, dz))]
    all_gather x8 -> x0, waiting for transfers between devices: 142 us -> none  [the longest x1 60.3 us: per_device(): lax.all_gather(shards[13], 'group', axis=0, tiled=True)]
    ppermute x0 -> x154, waiting for transfers between devices: none -> 137 us  [the longest x150 137 us: send(): lax.ppermute(v, ('ctx', 'group', 'replica'), self.perm(dx, dy, dc, dz))]
    convert_element_type x33 -> x5, other arithmetic: 114 us -> 2.73 us  [the longest x1 1.58 us: per_device(): g_wdown = jnp.concatenate(downs, 0).astype(F32)]
    reduce_sum x17 -> x0, other arithmetic: 73.3 us -> none  [the longest x2 42 us: one_block(): total = jnp.sum(jnp.exp(scores - top), -1, keepdims=True)]
  transfers between devices with their start and end apart: 15 -> 154, of which waited for: 8 -> 43; matrix products, arithmetic and copies ran while one was open for 27% -> 10% of each run, Pallas kernels for 0% -> 34%
where the time goes in v1:
time: 678 us; the launch traced here: 668 us
  Pallas kernels  277 us (41%)
  starting transfers between devices  163 us (24%)
  waiting for transfers between devices  137 us (20%)
  local copies, waits for them, and re-layouts  67.1 us (10%)
  other arithmetic  21.9 us (3%)
    ppermute x150, starting transfers between devices, send(): lax.ppermute(v, ('ctx', 'group', 'replica'), self.perm(dx, dy, dc, dz))  155 us
    ppermute x150, waiting for transfers between devices, send(): lax.ppermute(v, ('ctx', 'group', 'replica'), self.perm(dx, dy, dc, dz))  137 us
    pallas_call x3, Pallas kernels, attend_bwd(): pl.pallas_call(functools.partial(bwd_kernel, plan), in_specs=[SMEM] + [VM...  84.2 us
    pallas_call x2, Pallas kernels, mlp_part(): pl.pallas_call(body, in_specs=[SMEM, VMEM, VMEM, VMEM] + ([] if first els...  66.2 us
    pallas_call x3, Pallas kernels, attend_fwd(): pl.pallas_call(functools.partial(fwd_kernel, plan, chunk), in_specs=[SMEM...  47.7 us
    pallas_call x15, Pallas kernels, add_split(): pl.pallas_call(functools.partial(add_kernel, n), in_specs=[VMEM] * n, out...  31.9 us
    unnamed x185, local copies, waits for them, and re-layouts  20.3 us
    pallas_call x1, Pallas kernels, mid_back(): pl.pallas_call(functools.partial(mid_back_kernel, plan), in_specs=[SMEM]...  14.2 us
  transfers between devices with their start and end apart: 154, of which 43 were waited for; matrix products, arithmetic and copies ran while one was open for 10% of the time, Pallas kernels for 34%

profile of v1, /device:TPU:0, one launch (start us, length us, event | category | flops | bytes accessed | tf_op | source)
XLA Modules:
  0.0 668.3 jit_solution(14463855239540928688)
XLA Ops:
  4.8 3.5 concatenate.23
  31.0 10.3 %collective-permute-start.4 = (bf16[1024,768]{1,0:T(8,128)(2,1)S(1)}, bf16[1024,768]{1,0:T(8,128)(2,1)}, u32[]{:S(2)}, u32[]{:S(2)}) collective-permute-start(bf16[1024,768]{1,0:T(8,128)(2,1)S(1)} %broadcast_select_fusion.1.own_ref.pat_ref), channel_id=1, source_target_pairs={{0,1},{1,0},{2,3},{3,2},{4,5},{5,4},{6,7},{7,6},{8,9},{9,8},{10,11... | collective-permute-start | bytes 4718600 | tf_op jit(solution)/shard_map/ppermute | solution.py:108
  47.4 3.3 collective-permute-start.7
  65.7 6.4 collective-permute-start.48
  81.5 3.2 collective-permute-start.22
  90.1 5.8 shard_map.296.h_ref
  102.9 16.1 %shard_map.299 = (bf16[2,80,2048]{2,1,0:T(8,128)(2,1)}, bf16[2,80,2048]{2,1,0:T(8,128)(2,1)}, bf16[2,80,2048]{2,1,0:T(8,128)(2,1)}, bf16[128,2048]{1,0:T(8,128)(...) custom-call(s32[4]{0:T(128)} %pad_add_fusion.sc_ref, ...), custom_call_target="tpu_custom_call" | custom-call | flops 16000000000 | bytes 10000000 | tf_op jit(solution)/shard_map/pallas_call | solution.py:235
  120.4 15.7 %shard_map.298 = (bf16[2,80,2048]{2,1,0:T(8,128)(2,1)}, bf16[2,80,2048]{2,1,0:T(8,128)(2,1)}, bf16[2,80,2048]{2,1,0:T(8,128)(2,1)}, bf16[128,2048]{1,0:T(8,128)(...) custom-call(s32[4]{0:T(128)} %pad_add_fusion.sc_ref, ...), custom_call_target="tpu_custom_call" | custom-call | flops 16000000000 | bytes 10000000 | tf_op jit(solution)/shard_map/pallas_call | solution.py:235
  141.9 15.9 %shard_map.297 = (bf16[2,80,2048]{2,1,0:T(8,128)(2,1)}, bf16[2,80,2048]{2,1,0:T(8,128)(2,1)}, bf16[2,80,2048]{2,1,0:T(8,128)(2,1)}, bf16[128,2048]{1,0:T(8,128)(...) custom-call(s32[4]{0:T(128)} %pad_add_fusion.sc_ref, ...), custom_call_target="tpu_custom_call" | custom-call | flops 16000000000 | bytes 10000000 | tf_op jit(solution)/shard_map/pallas_call | solution.py:235
  157.8 19.7 %collective-permute-done.41.rest_4_ = bf16[4,4,48,384]{3,2,1,0:T(8,128)(2,1)} collective-permute-done((bf16[4,4,48,384]{3,2,1,0:T(8,128)(2,1)}, bf16[4,4,48,384]{3,2,1,0:T(8,128)(2,1)}, u32[]{:S(2)}, u32[]{:S(2)}) %collective-permute-start.41) | collective-permute-done | bytes 589856 | tf_op jit(solution)/shard_map/ppermute | solution.py:108
  177.5 7.0 %collective-permute-done.42.rest_5_ = bf16[4,4,48,384]{3,2,1,0:T(8,128)(2,1)} collective-permute-done((bf16[4,4,48,384]{3,2,1,0:T(8,128)(2,1)}, bf16[4,4,48,384]{3,2,1,0:T(8,128)(2,1)}, u32[]{:S(2)}, u32[]{:S(2)}) %collective-permute-start.42) | collective-permute-done | bytes 589856 | tf_op jit(solution)/shard_map/ppermute | solution.py:108
  189.8 8.3 %shard_map.300 = (f32[1024,768]{1,0:T(8,128)}, bf16[1024,768]{1,0:T(8,128)(2,1)}, bf16[2,768,384]{2,1,0:T(8,128)(2,1)}) custom-call(s32[4]{0:T(128)} %pad_add_fusion.sc_ref, bf16[1024,768]{1,0:T(8,128)(2,1)} %copy-done.2, f32[8,768]{1,0:T(8,128)} %concatenate.24.vec_ref.rest_1_.rest_2_, bf16[128,1024]{1,0:T(8,128)(2,1)} %get-tuple-element.123.refs_0_.own_ref, ...), custom_call_target="tpu_custom_call" | custom-call | flops 1207959552 | bytes 12000000 | tf_op jit(solution)/shard_map/pallas_call | solution.py:297
  198.1 3.4 collective-permute-done.51.rest_5_
  201.5 11.9 %collective-permute-done.52.rest_6_ = bf16[4,4,48,384]{3,2,1,0:T(8,128)(2,1)} collective-permute-done((bf16[4,4,48,384]{3,2,1,0:T(8,128)(2,1)}, bf16[4,4,48,384]{3,2,1,0:T(8,128)(2,1)}, u32[]{:S(2)}, u32[]{:S(2)}) %collective-permute-start.52) | collective-permute-done | bytes 589856 | tf_op jit(solution)/shard_map/ppermute | solution.py:108
  214.1 32.8 %shard_map.301 = (f32[1024,768]{1,0:T(8,128)}, f32[1024,768]{1,0:T(8,128)}, f32[4,384]{1,0:T(4,128)}, bf16[4,4,4,48,384]{4,3,2,1,0:T(8,128)(2,1)}, bf16[4,4,4,48,384]{4,3,2,1,0:T(8,128)(2,1)}) custom-call(s32[4]{0:T(128)} %pad_add_fusion.sc_ref, bf16[1024,768]{1,0:T(8,128)(2,1)} %get-tuple-element.129.h_ref, bf16[1024,768]{1,0:T(8,128)(2,1)} %broadcast_select_fusion.g_ref, ...), custom_call_target="tpu_custom_call" | custom-call | flops 14495514624 | bytes 24000000 | tf_op jit(solution)/shard_map/pallas_call | solution.py:408
  247.9 33.4 %shard_map.302 = (bf16[1024,768]{1,0:T(8,128)(2,1)}, f32[1024,768]{1,0:T(8,128)}, f32[4,384]{1,0:T(4,128)}, bf16[4,4,4,48,384]{4,3,2,1,0:T(8,128)(2,1)}, bf16[4,4,4,48,384]{4,3,2,1,0:T(8,128)(2,1)}) custom-call(s32[4]{0:T(128)} %pad_add_fusion.sc_ref, bf16[1024,768]{1,0:T(8,128)(2,1)} %get-tuple-element.129.h_ref, ...), custom_call_target="tpu_custom_call" | custom-call | flops 14495514624 | bytes 24000000 | tf_op jit(solution)/shard_map/pallas_call | solution.py:408
  281.4 14.2 %shard_map.303 = (f32[1024,768]{1,0:T(8,128)}, f32[8,768]{1,0:T(8,128)}, bf16[4,4,48,384]{3,2,1,0:T(8,128)(2,1)}, bf16[4,4,48,384]{3,2,1,0:T(8,128)(2,1)}, bf16[...) custom-call(s32[4]{0:T(128)} %pad_add_fusion.sc_ref, ...), custom_call_target="tpu_custom_call" | custom-call | flops 2415919104 | bytes 20000000 | tf_op jit(solution)/shard_map/pallas_call | solution.py:479
  298.7 27.9 %shard_map.304 = (bf16[384,2048]{1,0:T(8,128)(2,1)}, bf16[4,4,48,384]{3,2,1,0:T(8,128)(2,1)}, f32[384,128]{1,0:T(8,128)}, f32[64,128]{1,0:T(8,128)}) custom-call(s32[4]{0:T(128)} %pad_add_fusion.sc_ref, bf16[2048,768]{1,0:T(8,128)(2,1)} %shard_map.296.h_ref, bf16[2,80,2048]{2,1,0:T(8,128)(2,1)} %get-tuple-element.134.q_ref, ...), custom_call_target="tpu_custom_call" | custom-call | flops 40000000000 | bytes 12000000 | tf_op jit(solution)/shard_map/pallas_call | solution.py:573
  332.7 27.9 %shard_map.306 = (bf16[384,2048]{1,0:T(8,128)(2,1)}, bf16[4,4,48,384]{3,2,1,0:T(8,128)(2,1)}, f32[384,128]{1,0:T(8,128)}, f32[64,128]{1,0:T(8,128)}) custom-call(s32[4]{0:T(128)} %pad_add_fusion.sc_ref, bf16[2048,768]{1,0:T(8,128)(2,1)} %shard_map.296.h_ref, bf16[2,80,2048]{2,1,0:T(8,128)(2,1)} %get-tuple-element.156.q_ref, ...), custom_call_target="tpu_custom_call" | custom-call | flops 40000000000 | bytes 12000000 | tf_op jit(solution)/shard_map/pallas_call | solution.py:573
  365.2 28.3 %shard_map.305 = (bf16[384,2048]{1,0:T(8,128)(2,1)}, bf16[4,4,48,384]{3,2,1,0:T(8,128)(2,1)}, f32[384,128]{1,0:T(8,128)}, f32[64,128]{1,0:T(8,128)}) custom-call(s32[4]{0:T(128)} %pad_add_fusion.sc_ref, bf16[2048,768]{1,0:T(8,128)(2,1)} %shard_map.296.h_ref, bf16[2,80,2048]{2,1,0:T(8,128)(2,1)} %get-tuple-element.146.q_ref, ...), custom_call_target="tpu_custom_call" | custom-call | flops 40000000000 | bytes 12000000 | tf_op jit(solution)/shard_map/pallas_call | solution.py:573
  396.1 6.7 shard_map.307
  492.6 12.7 %collective-permute-done.120 = bf16[48,384]{1,0:T(8,128)(2,1)S(1)} collective-permute-done((bf16[48,384]{1,0:T(8,128)(2,1)}, bf16[48,384]{1,0:T(8,128)(2,1)S(1)}, u32[]{:S(2)}, u32[]{:S(2)}) %collective-permute-start.120) | collective-permute-done | bytes 36896 | tf_op jit(solution)/shard_map/ppermute | solution.py:108
  505.4 5.1 collective-permute-done.121
  517.2 11.5 %shard_map.308 = (f32[1024,768]{1,0:T(8,128)}, bf16[1024,768]{1,0:T(8,128)(2,1)}, f32[8,768]{1,0:T(8,128)}) custom-call(bf16[1024,768]{1,0:T(8,128)(2,1)} %collective-permute-done.61.rcv_ref, bf16[1024,768]{1,0:T(8,128)(2,1)} %copy-done.2, f32[1024,768]{1,0:T(8,128)} %get-tuple-element.169.dx_ref, f32[8,768]{1,0:T(8,128)} %concatenate.24.vec_ref.rest_1_.rest_2_, ...), custom_call_target="tpu_custom_call" | custom-call | flops 1811939328 | bytes 20000000 | tf_op jit(solution)/shard_map/pallas_call | solution.py:640
  534.6 3.7 collective-permute-done.105
  539.3 4.0 shard_map.321
  555.5 3.9 shard_map.318
  570.2 6.1 collective-permute-done.142.refs_2_
  576.3 12.5 %collective-permute-done.143.refs_3_ = bf16[4,4,48,384]{3,2,1,0:T(8,128)(2,1)} collective-permute-done((bf16[4,4,48,384]{3,2,1,0:T(8,128)(2,1)}, bf16[4,4,48,384]{3,2,1,0:T(8,128)(2,1)}, u32[]{:S(2)}, u32[]{:S(2)}) %collective-permute-start.143) | collective-permute-done | bytes 589856 | tf_op jit(solution)/shard_map/ppermute | solution.py:108
  596.1 5.4 collective-permute-done.128.refs_2_
  603.3 10.6 %collective-permute-done.129.refs_3_ = bf16[4,4,48,384]{3,2,1,0:T(8,128)(2,1)S(1)} collective-permute-done((bf16[4,4,48,384]{3,2,1,0:T(8,128)(2,1)}, bf16[4,4,48,384]{3,2,1,0:T(8,128)(2,1)S(1)}, u32[]{:S(2)}, u32[]{:S(2)}) %collective-permute-start.129) | collective-permute-done | bytes 589856 | tf_op jit(solution)/shard_map/ppermute | solution.py:108
  664.3 3.6 select_bitcast_fusion
  (629 shorter events, 284.7 us)
Async XLA Ops:
  31.0 57.2 %collective-permute-start.4 = (bf16[1024,768]{1,0:T(8,128)(2,1)S(1)}, bf16[1024,768]{1,0:T(8,128)(2,1)}, u32[]{:S(2)}, u32[]{:S(2)}) collective-permute-start(bf16[1024,768]{1,0:T(8,128)(2,1)S(1)} %broadcast_select_fusion.1.own_ref.pat_ref), channel_id=1, source_target_pairs={{0,1},{1,0},{2,3},{3,2},{4,5},{5,4},{6,7},{7,6},{8,9},{9,8},{10,11... | collective-permute-start | bytes 4718600 | tf_op jit(solution)/shard_map/ppermute | solution.py:108
  136.1 48.9 %collective-permute-start.36 = (bf16[1024,768]{1,0:T(8,128)(2,1)S(1)}, bf16[1024,768]{1,0:T(8,128)(2,1)}, u32[]{:S(2)}, u32[]{:S(2)}) collective-permute-start(bf16[1024,768]{1,0:T(8,128)(2,1)S(1)} %bitcast.306), channel_id=1, source_target_pairs={{1,16},{16,1},{3,18},{18,3},{5,20},{20,5},{7,22},{22,7},{9,24},{24... | collective-permute-start | bytes 4718600 | tf_op jit(solution)/shard_map/ppermute | solution.py:117
  137.9 39.5 %collective-permute-start.41 = (bf16[4,4,48,384]{3,2,1,0:T(8,128)(2,1)}, bf16[4,4,48,384]{3,2,1,0:T(8,128)(2,1)}, u32[]{:S(2)}, u32[]{:S(2)}) collective-permute-start(bf16[4,4,48,384]{3,2,1,0:T(8,128)(2,1)} %pad_maximum_fusion.rest_2_), channel_id=1, source_target_pairs={{0,16},{1,17},{2,18},{3,19},{4,20},{5,21},{6,22},{7,23},{8,24},{9,... | collective-permute-start | bytes 1769480 | tf_op jit(solution)/shard_map/ppermute | solution.py:108
  140.1 44.4 %collective-permute-start.42 = (bf16[4,4,48,384]{3,2,1,0:T(8,128)(2,1)}, bf16[4,4,48,384]{3,2,1,0:T(8,128)(2,1)}, u32[]{:S(2)}, u32[]{:S(2)}) collective-permute-start(bf16[4,4,48,384]{3,2,1,0:T(8,128)(2,1)} %pad_maximum_fusion.rest_2_), channel_id=1, source_target_pairs={{0,18},{1,19},{2,16},{3,17},{4,22},{5,23},{6,20},{7,21},{8,26},{9,... | collective-permute-start | bytes 1769480 | tf_op jit(solution)/shard_map/ppermute | solution.py:108
  141.2 43.3 %collective-permute-start.43 = (bf16[4,4,48,384]{3,2,1,0:T(8,128)(2,1)}, bf16[4,4,48,384]{3,2,1,0:T(8,128)(2,1)}, u32[]{:S(2)}, u32[]{:S(2)}) collective-permute-start(bf16[4,4,48,384]{3,2,1,0:T(8,128)(2,1)} %pad_maximum_fusion.rest_2_), channel_id=1, source_target_pairs={{0,1},{1,0},{2,3},{3,2},{4,5},{5,4},{6,7},{7,6},{8,9},{9,8},{10,11... | collective-permute-start | bytes 1769480 | tf_op jit(solution)/shard_map/ppermute | solution.py:108
  141.2 43.8 %collective-permute-start.50 = (bf16[4,4,48,384]{3,2,1,0:T(8,128)(2,1)}, bf16[4,4,48,384]{3,2,1,0:T(8,128)(2,1)}, u32[]{:S(2)}, u32[]{:S(2)}) collective-permute-start(bf16[4,4,48,384]{3,2,1,0:T(8,128)(2,1)} %pad_maximum_fusion.1.rest_3_), channel_id=1, source_target_pairs={{0,2},{1,3},{2,0},{3,1},{4,6},{5,7},{6,4},{7,5},{8,10},{9,11},{10,... | collective-permute-start | bytes 1769480 | tf_op jit(solution)/shard_map/ppermute | solution.py:108
  185.0 28.4 %collective-permute-start.52 = (bf16[4,4,48,384]{3,2,1,0:T(8,128)(2,1)}, bf16[4,4,48,384]{3,2,1,0:T(8,128)(2,1)}, u32[]{:S(2)}, u32[]{:S(2)}) collective-permute-start(bf16[4,4,48,384]{3,2,1,0:T(8,128)(2,1)} %pad_maximum_fusion.1.rest_3_), channel_id=1, source_target_pairs={{0,18},{1,19},{2,16},{3,17},{4,22},{5,23},{6,20},{7,21},{8,26},{9,... | collective-permute-start | bytes 1769480 | tf_op jit(solution)/shard_map/ppermute | solution.py:108
  187.3 26.7 %collective-permute-start.45 = (bf16[4,4,48,384]{3,2,1,0:T(8,128)(2,1)}, bf16[4,4,48,384]{3,2,1,0:T(8,128)(2,1)}, u32[]{:S(2)}, u32[]{:S(2)}) collective-permute-start(bf16[4,4,48,384]{3,2,1,0:T(8,128)(2,1)} %collective-permute-done.41.rest_4_), channel_id=1, source_target_pairs={{0,1},{1,0},{2,3},{3,2},{4,5},{5,4},{6,7},{7,6},{8,9},{9,8},{10,11... | collective-permute-start | bytes 1769480 | tf_op jit(solution)/shard_map/ppermute | solution.py:108
  187.8 26.3 %collective-permute-start.46 = (bf16[4,4,48,384]{3,2,1,0:T(8,128)(2,1)}, bf16[4,4,48,384]{3,2,1,0:T(8,128)(2,1)}, u32[]{:S(2)}, u32[]{:S(2)}) collective-permute-start(bf16[4,4,48,384]{3,2,1,0:T(8,128)(2,1)} %collective-permute-done.42.rest_5_), channel_id=1, source_target_pairs={{0,1},{1,0},{2,3},{3,2},{4,5},{5,4},{6,7},{7,6},{8,9},{9,8},{10,11... | collective-permute-start | bytes 1769480 | tf_op jit(solution)/shard_map/ppermute | solution.py:108
  201.5 45.4 %collective-permute-start.53 = (bf16[4,4,48,384]{3,2,1,0:T(8,128)(2,1)S(1)}, bf16[4,4,48,384]{3,2,1,0:T(8,128)(2,1)S(1)}, u32[]{:S(2)}, u32[]{:S(2)}) collective-permute-start(bf16[4,4,48,384]{3,2,1,0:T(8,128)(2,1)S(1)} %copy-done.7), channel_id=1, source_target_pairs={{0,1},{1,0},{2,3},{3,2},{4,5},{5,4},{6,7},{7,6},{8,9},{9,8},{10,11... | collective-permute-start | bytes 1769480 | tf_op jit(solution)/shard_map/ppermute | solution.py:108
  213.5 33.5 %collective-permute-start.54 = (bf16[4,4,48,384]{3,2,1,0:T(8,128)(2,1)}, bf16[4,4,48,384]{3,2,1,0:T(8,128)(2,1)S(1)}, u32[]{:S(2)}, u32[]{:S(2)}) collective-permute-start(bf16[4,4,48,384]{3,2,1,0:T(8,128)(2,1)} %collective-permute-done.50.rest_4_), channel_id=1, source_target_pairs={{0,1},{1,0},{2,3},{3,2},{4,5},{5,4},{6,7},{7,6},{8,9},{9,8},{10,11... | collective-permute-start | bytes 1769480 | tf_op jit(solution)/shard_map/ppermute | solution.py:108
  213.5 33.5 %collective-permute-start.55 = (bf16[4,4,48,384]{3,2,1,0:T(8,128)(2,1)}, bf16[4,4,48,384]{3,2,1,0:T(8,128)(2,1)}, u32[]{:S(2)}, u32[]{:S(2)}) collective-permute-start(bf16[4,4,48,384]{3,2,1,0:T(8,128)(2,1)} %collective-permute-done.51.rest_5_), channel_id=1, source_target_pairs={{0,1},{1,0},{2,3},{3,2},{4,5},{5,4},{6,7},{7,6},{8,9},{9,8},{10,11... | collective-permute-start | bytes 1769480 | tf_op jit(solution)/shard_map/ppermute | solution.py:108
  214.0 33.0 %collective-permute-start.56 = (bf16[4,4,48,384]{3,2,1,0:T(8,128)(2,1)}, bf16[4,4,48,384]{3,2,1,0:T(8,128)(2,1)}, u32[]{:S(2)}, u32[]{:S(2)}) collective-permute-start(bf16[4,4,48,384]{3,2,1,0:T(8,128)(2,1)} %collective-permute-done.52.rest_6_), channel_id=1, source_target_pairs={{0,1},{1,0},{2,3},{3,2},{4,5},{5,4},{6,7},{7,6},{8,9},{9,8},{10,11... | collective-permute-start | bytes 1769480 | tf_op jit(solution)/shard_map/ppermute | solution.py:108
  296.1 35.9 %collective-permute-start.60 = (bf16[128,1024]{1,0:T(8,128)(2,1)}, bf16[128,1024]{1,0:T(8,128)(2,1)S(1)}, u32[]{:S(2)}, u32[]{:S(2)}) collective-permute-start(bf16[128,1024]{1,0:T(8,128)(2,1)} %get-tuple-element.164), channel_id=1, source_target_pairs={{0,1},{1,0},{2,3},{3,2},{4,5},{5,4},{6,7},{7,6},{8,9},{9,8},{10,11... | collective-permute-start | bytes 786440 | tf_op jit(solution)/shard_map/ppermute | solution.py:108
  296.2 68.3 %collective-permute-start.59 = (bf16[128,1024]{1,0:T(8,128)(2,1)}, bf16[128,1024]{1,0:T(8,128)(2,1)S(1)}, u32[]{:S(2)}, u32[]{:S(2)}) collective-permute-start(bf16[128,1024]{1,0:T(8,128)(2,1)} %get-tuple-element.154), channel_id=1, source_target_pairs={{0,1},{1,0},{2,3},{3,2},{4,5},{5,4},{6,7},{7,6},{8,9},{9,8},{10,11... | collective-permute-start | bytes 786440 | tf_op jit(solution)/shard_map/ppermute | solution.py:108
  328.5 74.4 %collective-permute-start.63 = (bf16[4,48,384]{2,1,0:T(8,128)(2,1)S(1)}, bf16[4,48,384]{2,1,0:T(8,128)(2,1)S(1)}, u32[]{:S(2)}, u32[]{:S(2)}) collective-permute-start(bf16[4,48,384]{2,1,0:T(8,128)(2,1)S(1)} %get-tuple-element.239), channel_id=1, source_target_pairs={{0,2},{1,3},{2,0},{3,1},{4,6},{5,7},{6,4},{7,5},{8,10},{9,11},{10,... | collective-permute-start | bytes 442376 | tf_op jit(solution)/shard_map/ppermute | solution.py:108
  329.8 74.7 %collective-permute-start.64 = (bf16[4,48,384]{2,1,0:T(8,128)(2,1)S(1)}, bf16[4,48,384]{2,1,0:T(8,128)(2,1)}, u32[]{:S(2)}, u32[]{:S(2)}) collective-permute-start(bf16[4,48,384]{2,1,0:T(8,128)(2,1)S(1)} %get-tuple-element.238), channel_id=1, source_target_pairs={{0,16},{1,17},{2,18},{3,19},{4,20},{5,21},{6,22},{7,23},{8,24},{9,... | collective-permute-start | bytes 442376 | tf_op jit(solution)/shard_map/ppermute | solution.py:108
  330.1 75.8 %collective-permute-start.65 = (bf16[4,48,384]{2,1,0:T(8,128)(2,1)S(1)}, bf16[4,48,384]{2,1,0:T(8,128)(2,1)}, u32[]{:S(2)}, u32[]{:S(2)}) collective-permute-start(bf16[4,48,384]{2,1,0:T(8,128)(2,1)S(1)} %get-tuple-element.237), channel_id=1, source_target_pairs={{0,18},{1,19},{2,16},{3,17},{4,22},{5,23},{6,20},{7,21},{8,26},{9,... | collective-permute-start | bytes 442376 | tf_op jit(solution)/shard_map/ppermute | solution.py:108
  362.5 44.2 %collective-permute-start.89 = (bf16[4,48,384]{2,1,0:T(8,128)(2,1)S(1)}, bf16[4,48,384]{2,1,0:T(8,128)(2,1)S(1)}, u32[]{:S(2)}, u32[]{:S(2)}) collective-permute-start(bf16[4,48,384]{2,1,0:T(8,128)(2,1)S(1)} %get-tuple-element.247), channel_id=1, source_target_pairs={{0,2},{1,3},{2,0},{3,1},{4,6},{5,7},{6,4},{7,5},{8,10},{9,11},{10,... | collective-permute-start | bytes 442376 | tf_op jit(solution)/shard_map/ppermute | solution.py:108
  364.5 46.2 %collective-permute-start.90 = (bf16[4,48,384]{2,1,0:T(8,128)(2,1)S(1)}, bf16[4,48,384]{2,1,0:T(8,128)(2,1)}, u32[]{:S(2)}, u32[]{:S(2)}) collective-permute-start(bf16[4,48,384]{2,1,0:T(8,128)(2,1)S(1)} %get-tuple-element.246), channel_id=1, source_target_pairs={{0,16},{1,17},{2,18},{3,19},{4,20},{5,21},{6,22},{7,23},{8,24},{9,... | collective-permute-start | bytes 442376 | tf_op jit(solution)/shard_map/ppermute | solution.py:108
  422.1 116.2 %collective-permute-start.140 = (bf16[4,4,4,48,384]{4,3,2,1,0:T(8,128)(2,1)}, bf16[4,4,4,48,384]{4,3,2,1,0:T(8,128)(2,1)}, u32[]{:S(2)}, u32[]{:S(2)}) collective-permute-start(bf16[4,4,4,48,384]{4,3,2,1,0:T(8,128)(2,1)} %get-tuple-element.218), channel_id=1, source_target_pairs={{0,1},{1,0},{2,3},{3,2},{4,5},{5,4},{6,7},{7,6},{8,9},{9,8},{10,11... | collective-permute-start | bytes 7077896 | tf_op jit(solution)/shard_map/ppermute | solution.py:108
  422.2 38.7 %collective-permute-start.112 = (bf16[4,4,48,384]{3,2,1,0:T(8,128)(2,1)}, bf16[4,4,48,384]{3,2,1,0:T(8,128)(2,1)S(1)}, u32[]{:S(2)}, u32[]{:S(2)}) collective-permute-start(bf16[4,4,48,384]{3,2,1,0:T(8,128)(2,1)} %get-tuple-element.198), channel_id=1, source_target_pairs={{0,1},{1,0},{2,3},{3,2},{4,5},{5,4},{6,7},{7,6},{8,9},{9,8},{10,11... | collective-permute-start | bytes 1769480 | tf_op jit(solution)/shard_map/ppermute | solution.py:108
  470.0 82.4 %collective-permute-start.126 = (bf16[4,4,4,48,384]{4,3,2,1,0:T(8,128)(2,1)}, bf16[4,4,4,48,384]{4,3,2,1,0:T(8,128)(2,1)}, u32[]{:S(2)}, u32[]{:S(2)}) collective-permute-start(bf16[4,4,4,48,384]{4,3,2,1,0:T(8,128)(2,1)} %get-tuple-element.208), channel_id=1, source_target_pairs={{0,1},{1,0},{2,3},{3,2},{4,5},{5,4},{6,7},{7,6},{8,9},{9,8},{10,11... | collective-permute-start | bytes 7077896 | tf_op jit(solution)/shard_map/ppermute | solution.py:108
  482.9 76.5 %collective-permute-start.57 = (bf16[1024,768]{1,0:T(8,128)(2,1)}, bf16[1024,768]{1,0:T(8,128)(2,1)}, u32[]{:S(2)}, u32[]{:S(2)}) collective-permute-start(bf16[1024,768]{1,0:T(8,128)(2,1)} %get-tuple-element.133), channel_id=1, source_target_pairs={{1,16},{16,1},{3,18},{18,3},{5,20},{20,5},{7,22},{22,7},{9,24},{24... | collective-permute-start | bytes 4718600 | tf_op jit(solution)/shard_map/ppermute | solution.py:117
  484.9 32.2 %collective-permute-start.61 = (bf16[1024,768]{1,0:T(8,128)(2,1)}, bf16[1024,768]{1,0:T(8,128)(2,1)}, u32[]{:S(2)}, u32[]{:S(2)}) collective-permute-start(bf16[1024,768]{1,0:T(8,128)(2,1)} %shard_map.307), channel_id=1, source_target_pairs={{0,1},{1,0},{2,3},{3,2},{4,5},{5,4},{6,7},{7,6},{8,9},{9,8},{10,11... | collective-permute-start | bytes 4718600 | tf_op jit(solution)/shard_map/ppermute | solution.py:108
  561.8 27.0 %collective-permute-start.143 = (bf16[4,4,48,384]{3,2,1,0:T(8,128)(2,1)}, bf16[4,4,48,384]{3,2,1,0:T(8,128)(2,1)}, u32[]{:S(2)}, u32[]{:S(2)}) collective-permute-start(bf16[4,4,48,384]{3,2,1,0:T(8,128)(2,1)} %get-tuple-element.222), channel_id=1, source_target_pairs={{0,18},{1,19},{2,16},{3,17},{4,22},{5,23},{6,20},{7,21},{8,26},{9,... | collective-permute-start | bytes 1769480 | tf_op jit(solution)/shard_map/ppermute | solution.py:108
  562.1 30.4 %collective-permute-start.127 = (bf16[4,4,48,384]{3,2,1,0:T(8,128)(2,1)}, bf16[4,4,48,384]{3,2,1,0:T(8,128)(2,1)S(1)}, u32[]{:S(2)}, u32[]{:S(2)}) collective-permute-start(bf16[4,4,48,384]{3,2,1,0:T(8,128)(2,1)} %get-tuple-element.210), channel_id=1, source_target_pairs={{0,2},{1,3},{2,0},{3,1},{4,6},{5,7},{6,4},{7,5},{8,10},{9,11},{10,... | collective-permute-start | bytes 1769480 | tf_op jit(solution)/shard_map/ppermute | solution.py:108
  566.0 35.4 %collective-permute-start.128 = (bf16[4,4,48,384]{3,2,1,0:T(8,128)(2,1)}, bf16[4,4,48,384]{3,2,1,0:T(8,128)(2,1)S(1)}, u32[]{:S(2)}, u32[]{:S(2)}) collective-permute-start(bf16[4,4,48,384]{3,2,1,0:T(8,128)(2,1)} %get-tuple-element.211), channel_id=1, source_target_pairs={{0,16},{1,17},{2,18},{3,19},{4,20},{5,21},{6,22},{7,23},{8,24},{9,... | collective-permute-start | bytes 1769480 | tf_op jit(solution)/shard_map/ppermute | solution.py:108
  568.0 45.9 %collective-permute-start.129 = (bf16[4,4,48,384]{3,2,1,0:T(8,128)(2,1)}, bf16[4,4,48,384]{3,2,1,0:T(8,128)(2,1)S(1)}, u32[]{:S(2)}, u32[]{:S(2)}) collective-permute-start(bf16[4,4,48,384]{3,2,1,0:T(8,128)(2,1)} %get-tuple-element.212), channel_id=1, source_target_pairs={{0,18},{1,19},{2,16},{3,17},{4,22},{5,23},{6,20},{7,21},{8,26},{9,... | collective-permute-start | bytes 1769480 | tf_op jit(solution)/shard_map/ppermute | solution.py:108
  591.3 27.3 %collective-permute-start.145 = (bf16[4,48,384]{2,1,0:T(8,128)(2,1)}, bf16[4,48,384]{2,1,0:T(8,128)(2,1)}, u32[]{:S(2)}, u32[]{:S(2)}) collective-permute-start(bf16[4,48,384]{2,1,0:T(8,128)(2,1)} %get-tuple-element.225), channel_id=1, source_target_pairs={{0,8},{1,9},{2,10},{3,11},{4,12},{5,13},{6,14},{7,15},{8,0},{9,1},... | collective-permute-start | bytes 442376 | tf_op jit(solution)/shard_map/ppermute | solution.py:108
  592.6 28.9 %collective-permute-start.146 = (bf16[4,48,384]{2,1,0:T(8,128)(2,1)}, bf16[4,48,384]{2,1,0:T(8,128)(2,1)}, u32[]{:S(2)}, u32[]{:S(2)}) collective-permute-start(bf16[4,48,384]{2,1,0:T(8,128)(2,1)} %get-tuple-element.226), channel_id=1, source_target_pairs={{0,12},{1,13},{2,14},{3,15},{4,0},{5,1},{6,2},{7,3},{8,4},{9,5},{1... | collective-permute-start | bytes 442376 | tf_op jit(solution)/shard_map/ppermute | solution.py:108
  601.5 61.6 %collective-permute-start.62 = (bf16[1024,768]{1,0:T(8,128)(2,1)}, bf16[1024,768]{1,0:T(8,128)(2,1)}, u32[]{:S(2)}, u32[]{:S(2)}) collective-permute-start(bf16[1024,768]{1,0:T(8,128)(2,1)} %get-tuple-element.171), channel_id=1, source_target_pairs={{1,16},{16,1},{3,18},{18,3},{5,20},{20,5},{7,22},{22,7},{9,24},{24... | collective-permute-start | bytes 4718600 | tf_op jit(solution)/shard_map/ppermute | solution.py:117
  (190 other events, 1681.9 us)
